TPU v7x, 1024 devices: a whole 8x8x8 slice. The times are simulated.
1024 devices in a mesh: grp: 4 (over x_lo), gx: 8 (over z), gy: 32 (over x_hi, y, core).
Axes of the slice: x: 8 (x_hi: 2, x_lo: 4; x = x_hi * 4 + x_lo), y: 8, z: 8, core: 2. Of those that a mesh axis runs over, the one named last changes fastest.
Arguments:
- zonal_boundary_speed: float32 [32, 32, 4, 1024], P(None, 'gy', 'grp', 'gx'), may hold values from -0.2 to 0.2
- meridional_boundary_speed: float32 [32, 32, 4, 1024], P(None, 'gy', 'grp', 'gx'), may hold values from -0.2 to 0.2
- potential_warmth: float32 [32, 32, 4, 1024], P(None, 'gy', 'grp', 'gx'), may hold values from 2 to 28
- saltiness_field: float32 [32, 32, 4, 1024], P(None, 'gy', 'grp', 'gx'), may hold values from 33 to 37
- quiescent_mixing_profile: float32 [32, 32, 4, 1024], P(None, 'gy', 'grp', 'gx'), may hold values from 0.005 to 0.05
- substance_amounts: float32 [19, 32, 128, 1024], P(None, 'grp', 'gy', 'gx'), may hold values from 0.1 to 3
- submerged_layer_number: int32 [128, 1024], P('gy', 'gx'), may hold values from 0 to 32
- solar_radiation: float32 [128, 1024], P('gy', 'gx'), may hold values from 0.2 to 1
- interaction_rates: float32 [19, 19], replicated, may hold values from -1.25 to 1.25
- photosynthetic_rates: float32 [19], replicated, may hold values from 0.1 to 1
- saturation_irradiance: float32 [19], replicated, may hold values from 0.05 to 0.5
- pigment_per_tracer: float32 [19], replicated, may hold values from 0.01 to 0.1
Outputs:
- east_final: float32 [32, 32, 4, 1024], P(None, 'gy', 'grp', 'gx')
- north_final: float32 [32, 32, 4, 1024], P(None, 'gy', 'grp', 'gx')
- temperature_final: float32 [32, 32, 4, 1024], P(None, 'gy', 'grp', 'gx')
- salinity_final: float32 [32, 32, 4, 1024], P(None, 'gy', 'grp', 'gx')
- tracers_final: float32 [19, 32, 128, 1024], P(None, 'grp', 'gy', 'gx')
All inputs are finite; a program needn't handle non-finite values.
Results may differ from a plain program's by a relative error of at most 0.0001.
Values sent between devices are 32-bit elements; how exact they have to be, the bound alone decides.
A program may use at most 32 MiB of HBM per device.

v0:
```python
import jax
import jax.numpy as jnp
from jax import lax
from jax.sharding import PartitionSpec as P

STEPS = 2


WATER_ATTEN = 0.01
PIGMENT_ATTEN = 0.05
WARMING_UPTAKE = 5.0
WARM_EXPANSION = 0.2
SALT_EXPANSION = 0.8
CONVECT_MIX = 0.15
SIDE_DIFFUSE = 0.05
WARMING_FACTOR = 0.0633
TIME_STEP = 0.5


def with_halo(cells, sides, width):
    for axis, dim in sides:
        count = lax.axis_size(axis)
        ends = count - 1
        head = lax.slice_in_dim(cells, 0, width, axis=dim)
        tail = lax.slice_in_dim(cells, cells.shape[dim] - width, cells.shape[dim], axis=dim)
        cells = jnp.concatenate(
            [
                lax.ppermute(tail, axis, [(i, (i + 1) % count) for i in range(ends)]),
                cells,
                lax.ppermute(head, axis, [((i + 1) % count, i) for i in range(ends)]),
            ],
            axis=dim,
        )
    return cells


def trim_axis(values, dimension_slot, start, stop):
    leading = (slice(None),) * (values.ndim + dimension_slot)
    return values[leading + (slice(start, stop),)]


def face_divergence(tracer_amounts, velocity, submerged_mask, dimension_slot):
    lower_conc = trim_axis(tracer_amounts, dimension_slot, None, -1)
    upper_conc = trim_axis(tracer_amounts, dimension_slot, 1, None)
    face_speed = trim_axis(velocity, dimension_slot, None, -1)
    opening = trim_axis(submerged_mask, dimension_slot, None, -1) * trim_axis(
        submerged_mask, dimension_slot, 1, None
    )
    flux_face = opening * (
        jnp.maximum(face_speed, 0.0) * lower_conc
        + jnp.minimum(face_speed, 0.0) * upper_conc
        - SIDE_DIFFUSE * (upper_conc - lower_conc)
    )
    return trim_axis(flux_face, dimension_slot, 1, None) - trim_axis(
        flux_face, dimension_slot, None, -1
    )


def level_divergence(tracer_amounts, mixing_coefficient):
    flux_face = trim_axis(mixing_coefficient, -3, None, -1) * (
        trim_axis(tracer_amounts, -3, 1, None) - trim_axis(tracer_amounts, -3, None, -1)
    )
    return trim_axis(flux_face, -3, 1, None) - trim_axis(flux_face, -3, None, -1)


def light_columns(pigment, surface):
    attenuation = WATER_ATTEN + PIGMENT_ATTEN * pigment
    above = jnp.cumsum(attenuation, axis=0) - attenuation
    top_light = surface * jnp.exp(-above)
    return (top_light * (1.0 - jnp.exp(-attenuation)), top_light * jnp.exp(-0.5 * attenuation))


def marine_advance(
    zonal_transport,
    meridional_transport,
    thermal_mesh,
    brine_values,
    quiescent_mixing,
    radiative_warming,
    submerged_mask,
):
    thermal_mesh = thermal_mesh + WARMING_UPTAKE * radiative_warming * submerged_mask
    water_buoyancy = SALT_EXPANSION * brine_values - WARM_EXPANSION * thermal_mesh
    strat = water_buoyancy[1:] - water_buoyancy[:-1]
    face_mix = (
        0.5 * (quiescent_mixing[:-1] + quiescent_mixing[1:]) + CONVECT_MIX * jax.nn.sigmoid(-strat)
    ) * submerged_mask[1:]
    bottom = jnp.zeros_like(face_mix[:1])
    mixing_coefficient = jnp.concatenate([face_mix, bottom], axis=0)

    def turbulent_stirring(field):
        flux_face = face_mix * (field[1:] - field[:-1])
        return (
            field
            + jnp.concatenate([flux_face, bottom], axis=0)
            - jnp.concatenate([bottom, flux_face], axis=0)
        )

    return (
        turbulent_stirring(zonal_transport),
        turbulent_stirring(meridional_transport),
        turbulent_stirring(thermal_mesh),
        turbulent_stirring(brine_values),
        mixing_coefficient,
    )


def chemical_kinetics(
    tracer_amounts,
    thermal_mesh,
    photosynthetic_radiance,
    submerged_mask,
    interaction_rates,
    photosynthetic_rates,
    saturation_irradiance,
):
    thermal_multiplier = jnp.exp(WARMING_FACTOR * (thermal_mesh - 20.0))
    mixed_terms = jnp.einsum(
        "ij,jzyx->izyx", interaction_rates, tracer_amounts, precision=lax.Precision.HIGHEST
    )
    light_limit = photosynthetic_radiance / (
        photosynthetic_radiance + saturation_irradiance[:, None, None, None]
    )
    return (
        TIME_STEP
        * submerged_mask
        * (
            thermal_multiplier * mixed_terms
            + photosynthetic_rates[:, None, None, None] * light_limit * tracer_amounts
        )
    )


def per_device(
    zonal_boundary_speed,
    meridional_boundary_speed,
    potential_warmth,
    saltiness_field,
    quiescent_mixing_profile,
    substance_amounts,
    submerged_layer_number,
    solar_radiation,
    interaction_rates,
    photosynthetic_rates,
    saturation_irradiance,
    pigment_per_tracer,
):
    member = lax.axis_index("grp")
    result_dimensions = zonal_boundary_speed.shape
    vertical_span = (result_dimensions[0], result_dimensions[2], result_dimensions[3])
    strip_rows = result_dimensions[2]
    band_levels = substance_amounts.shape[1]
    tracer_count = substance_amounts.shape[0]
    zonal_transport = zonal_boundary_speed.reshape(vertical_span)
    meridional_transport = meridional_boundary_speed.reshape(vertical_span)
    thermal_mesh = potential_warmth.reshape(vertical_span)
    brine_values = saltiness_field.reshape(vertical_span)
    quiescent_mixing = quiescent_mixing_profile.reshape(vertical_span)
    depth_strip = lax.dynamic_slice_in_dim(
        submerged_layer_number, member * strip_rows, strip_rows, 0
    )
    light_strip = lax.dynamic_slice_in_dim(solar_radiation, member * strip_rows, strip_rows, 0)
    marine_profiles = (
        lax.broadcasted_iota(jnp.int32, vertical_span, 0) < depth_strip[None]
    ).astype(jnp.float32)
    band_index = member * band_levels + lax.broadcasted_iota(
        jnp.int32, substance_amounts.shape[1:], 0
    )
    wet_band = (band_index < submerged_layer_number[None]).astype(jnp.float32)
    tracer_amounts = substance_amounts
    for repeat in range(STEPS):
        pigment_band = jnp.einsum(
            "i,izyx->zyx", pigment_per_tracer, tracer_amounts, precision=lax.Precision.HIGHEST
        )
        pigment_cols = lax.all_to_all(pigment_band, "grp", split_axis=1, concat_axis=0, tiled=True)
        radiative_warming, irradiance_profiles = light_columns(pigment_cols, light_strip[None])
        zonal_transport, meridional_transport, thermal_mesh, brine_values, mixing_coefficient = (
            marine_advance(
                zonal_transport,
                meridional_transport,
                thermal_mesh,
                brine_values,
                quiescent_mixing,
                radiative_warming,
                marine_profiles,
            )
        )
        stacked = jnp.stack(
            [
                zonal_transport,
                meridional_transport,
                thermal_mesh,
                mixing_coefficient,
                irradiance_profiles,
            ],
            axis=0,
        )
        forcing = lax.all_to_all(stacked, "grp", split_axis=1, concat_axis=2, tiled=True)
        band_east = forcing[0]
        band_north = forcing[1]
        band_temp = forcing[2]
        band_diff = forcing[3]
        band_par = forcing[4]
        joined = jnp.concatenate(
            [tracer_amounts, band_east[None], band_north[None], wet_band[None], band_diff[None]],
            axis=0,
        )
        padded = with_halo(joined, (("grp", 1), ("gx", 3), ("gy", 2)), 1)
        across_east = padded[:, 1:-1, 1:-1, :]
        across_north = padded[:, 1:-1, :, 1:-1]
        across_levels = padded[:, :, 1:-1, 1:-1]
        level_conc = across_levels[:tracer_count]
        level_diff = across_levels[tracer_count + 3]
        zonal_increment = face_divergence(
            across_east[:tracer_count], across_east[tracer_count], across_east[tracer_count + 2], -1
        )
        meridional_increment = face_divergence(
            across_north[:tracer_count],
            across_north[tracer_count + 1],
            across_north[tracer_count + 2],
            -2,
        )
        depthwise_transfer = level_divergence(level_conc, level_diff)
        tracer_amounts = (
            tracer_amounts
            - zonal_increment
            - meridional_increment
            + depthwise_transfer
            + chemical_kinetics(
                tracer_amounts,
                band_temp,
                band_par,
                wet_band,
                interaction_rates,
                photosynthetic_rates,
                saturation_irradiance,
            )
        )
    return (
        zonal_transport.reshape(result_dimensions),
        meridional_transport.reshape(result_dimensions),
        thermal_mesh.reshape(result_dimensions),
        brine_values.reshape(result_dimensions),
        tracer_amounts,
    )


def solution(mesh):
    placed = (
        P(None, "gy", "grp", "gx"),
        P(None, "gy", "grp", "gx"),
        P(None, "gy", "grp", "gx"),
        P(None, "gy", "grp", "gx"),
        P(None, "gy", "grp", "gx"),
        P(None, "grp", "gy", "gx"),
        P("gy", "gx"),
        P("gy", "gx"),
        P(),
        P(),
        P(),
        P(),
    )
    return jax.shard_map(
        per_device,
        mesh=mesh,
        in_specs=placed,
        out_specs=(
            P(None, "gy", "grp", "gx"),
            P(None, "gy", "grp", "gx"),
            P(None, "gy", "grp", "gx"),
            P(None, "gy", "grp", "gx"),
            P(None, "grp", "gy", "gx"),
        ),
        check_vma=False,
    )
```

profile of v0, /device:TPU:501, one launch (start us, length us, event | category | flops | bytes accessed | tf_op | source)
XLA Modules:
  0.0 134.7 jit_solution(15945735695244439217)
XLA Ops:
  0.7 1.5 %fusion.18 = f32[1,8,4,128]{3,0,2,1:T(1,128)S(1)} fusion(f32[19,8,4,128]{3,2,1,0:T(4,128)} %param.17, f32[19]{0:T(128)} %param.23), kind=kOutput, calls=%fused_computation.79 | convolution fusion | flops 933888 | bytes 327756 | tf_op jit(solution)/shard_map/i,izyx->zyx/dot_general | solution.py:172
  2.2 0.6 copy.168
  2.8 4.6 %all-to-all-start = ((f32[8,4,128]{2,0,1:T(8,128)}), f32[8,4,128]{2,0,1:T(8,128)S(1)}, u32[]{:S(2)}, u32[]{:S(2)}) async-start(f32[8,4,128]{2,0,1:T(8,128)} %bitcast.254), calls=%async_computation | async-start | bytes 32768 | tf_op jit(solution)/shard_map/all_to_all | solution.py:175
  7.4 0.7 dynamic-slice_bitcast_fusion
  8.1 0.2 copy.111
  8.3 1.8 %all-to-all-done = f32[8,4,128]{2,0,1:T(8,128)S(1)} async-done(((f32[8,4,128]{2,0,1:T(8,128)}), f32[8,4,128]{2,0,1:T(8,128)S(1)}, u32[]{:S(2)}, u32[]{:S(2)}) %all-to-all-start) | async-done | bytes 16416 | tf_op jit(solution)/shard_map/all_to_all | solution.py:175
  10.1 0.7 copy-done.2
  10.8 0.7 copy-done.3
  11.6 0.7 copy-done.4
  12.4 0.7 copy.100
  13.1 5.0 %all-to-all-start.1 = ((f32[5,32,1,128]{3,2,0,1:T(1,128)}), f32[5,32,1,128]{3,2,0,1:T(1,128)S(1)}, u32[]{:S(2)}, u32[]{:S(2)}) async-start(f32[5,32,1,128]{3,2,0,1:T(1,128)} %copy.100), calls=%async_computation.1 | async-start | bytes 163840 | tf_op jit(solution)/shard_map/all_to_all | solution.py:198
  18.2 2.7 %all-to-all-done.1 = f32[5,32,1,128]{3,2,0,1:T(1,128)S(1)} async-done(((f32[5,32,1,128]{3,2,0,1:T(1,128)}), f32[5,32,1,128]{3,2,0,1:T(1,128)S(1)}, u32[]{:S(2)}, u32[]{:S(2)}) %all-to-all-start.1) | async-done | bytes 81952 | tf_op jit(solution)/shard_map/all_to_all | solution.py:198
  20.9 0.2 concatenate.125
  21.2 2.6 %collective-permute-start = (f32[23,1,4,128]{3,0,2,1:T(8,128)S(1)}, f32[23,1,4,128]{3,0,2,1:T(8,128)S(1)}, u32[]{:S(2)}, u32[]{:S(2)}) collective-permute-start(f32[23,1,4,128]{3,0,2,1:T(8,128)S(1)} %get-tuple-element.60), channel_id=1, source_target_pairs={{0,256},{256,512},{512,768},{1,257},{257,513},{513,769},{2,258},{2... | collective-permute-start | bytes 141320 | tf_op jit(solution)/shard_map/ppermute | solution.py:28
  23.8 2.7 %collective-permute-start.1 = (f32[23,1,4,128]{3,0,2,1:T(8,128)S(1)}, f32[23,1,4,128]{3,0,2,1:T(8,128)S(1)}, u32[]{:S(2)}, u32[]{:S(2)}) collective-permute-start(f32[23,1,4,128]{3,0,2,1:T(8,128)S(1)} %get-tuple-element.59), channel_id=1, source_target_pairs={{256,0},{512,256},{768,512},{257,1},{513,257},{769,513},{258,2},{5... | collective-permute-start | bytes 141320 | tf_op jit(solution)/shard_map/ppermute | solution.py:30
  26.6 2.0 %collective-permute-done.1 = f32[23,1,4,128]{3,0,2,1:T(8,128)S(1)} collective-permute-done((f32[23,1,4,128]{3,0,2,1:T(8,128)S(1)}, f32[23,1,4,128]{3,0,2,1:T(8,128)S(1)}, u32[]{:S(2)}, u32[]{:S(2)}) %collective-permute-start.1) | collective-permute-done | bytes 47136 | tf_op jit(solution)/shard_map/ppermute | solution.py:30
  28.6 0.2 fusion.91
  28.8 1.9 %collective-permute-start.3 = (f32[23,10,4,1]{3,0,2,1:T(8,128)S(1)}, f32[23,10,4,1]{3,0,2,1:T(8,128)S(1)}, u32[]{:S(2)}, u32[]{:S(2)}) collective-permute-start(f32[23,10,4,1]{3,0,2,1:T(8,128)S(1)} %get-tuple-element.54), channel_id=1, source_target_pairs={{32,0},{64,32},{96,64},{128,96},{160,128},{192,160},{224,192},{33,... | collective-permute-start | bytes 11048 | tf_op jit(solution)/shard_map/ppermute | solution.py:30
  30.8 6.1 %collective-permute-start.2 = (f32[23,10,4,1]{3,0,2,1:T(8,128)S(1)}, f32[23,10,4,1]{3,0,2,1:T(8,128)S(1)}, u32[]{:S(2)}, u32[]{:S(2)}) collective-permute-start(f32[23,10,4,1]{3,0,2,1:T(8,128)S(1)} %get-tuple-element.53), channel_id=1, source_target_pairs={{0,32},{32,64},{64,96},{96,128},{128,160},{160,192},{192,224},{1,3... | collective-permute-start | bytes 11048 | tf_op jit(solution)/shard_map/ppermute | solution.py:28
  37.0 5.2 %collective-permute-done.3 = f32[23,10,4,1]{3,0,2,1:T(8,128)S(1)} collective-permute-done((f32[23,10,4,1]{3,0,2,1:T(8,128)S(1)}, f32[23,10,4,1]{3,0,2,1:T(8,128)S(1)}, u32[]{:S(2)}, u32[]{:S(2)}) %collective-permute-start.3) | collective-permute-done | bytes 3712 | tf_op jit(solution)/shard_map/ppermute | solution.py:30
  42.2 0.9 collective-permute-done.2
  43.1 0.3 pad_maximum_fusion.38
  43.3 7.2 %collective-permute-start.5 = (f32[23,10,1,130]{3,0,2,1:T(8,128)S(1)}, f32[23,10,1,130]{3,0,2,1:T(8,128)S(1)}, u32[]{:S(2)}, u32[]{:S(2)}) collective-permute-start(f32[23,10,1,130]{3,0,2,1:T(8,128)S(1)} %get-tuple-element.48), channel_id=1, source_target_pairs={{1,0},{2,1},{3,2},{4,3},{5,4},{6,5},{7,6},{8,7},{9,8},{10,9},{11,1... | collective-permute-start | bytes 358808 | tf_op jit(solution)/shard_map/ppermute | solution.py:30
  50.5 4.4 %collective-permute-start.4 = (f32[23,10,1,130]{3,0,2,1:T(8,128)S(1)}, f32[23,10,1,130]{3,0,2,1:T(8,128)S(1)}, u32[]{:S(2)}, u32[]{:S(2)}) collective-permute-start(f32[23,10,1,130]{3,0,2,1:T(8,128)S(1)} %get-tuple-element.47), channel_id=1, source_target_pairs={{0,1},{1,2},{2,3},{3,4},{4,5},{5,6},{6,7},{7,8},{8,9},{9,10},{10,1... | collective-permute-start | bytes 358808 | tf_op jit(solution)/shard_map/ppermute | solution.py:28
  54.9 0.3 pad_maximum_fusion.47
  55.3 0.4 subtract_multiply_fusion.1
  55.7 3.8 %collective-permute-done.5 = f32[23,10,1,130]{3,0,2,1:T(8,128)S(1)} collective-permute-done((f32[23,10,1,130]{3,0,2,1:T(8,128)S(1)}, f32[23,10,1,130]{3,0,2,1:T(8,128)S(1)}, u32[]{:S(2)}, u32[]{:S(2)}) %collective-permute-start.5) | collective-permute-done | bytes 119632 | tf_op jit(solution)/shard_map/ppermute | solution.py:30
  59.5 1.2 collective-permute-done.4
  60.7 0.2 pad_maximum_fusion.54
  60.9 0.3 subtract_multiply_fusion.2
  61.3 0.6 copy-done.9
  61.9 0.9 fusion.3
  62.9 0.3 fusion.83
  63.2 5.9 %all_to_all.48 = f32[8,4,128]{2,0,1:T(8,128)S(1)} all-to-all(f32[8,4,128]{2,0,1:T(8,128)S(1)} %bitcast.276), channel_id=1, replica_groups=mesh['grp'=4,'gx'=8,'gy'=32] {'grp'}, dimensions={1} | all-to-all | bytes 32768 | tf_op jit(solution)/shard_map/all_to_all | solution.py:175
  69.2 0.6 constant_dynamic-update-slice_fusion.9
  69.8 0.6 constant_dynamic-update-slice_fusion.8
  70.4 0.6 constant_dynamic-update-slice_fusion.7
  71.1 0.1 copy.115
  71.2 7.6 %all_to_all.49 = f32[5,32,1,128]{3,2,0,1:T(1,128)S(1)} all-to-all(f32[5,32,1,128]{3,2,0,1:T(1,128)S(1)} %copy.115), channel_id=1, replica_groups=mesh['grp'=4,'gx'=8,'gy'=32] {'grp'}, dimensions={1} | all-to-all | bytes 163840 | tf_op jit(solution)/shard_map/all_to_all | solution.py:198
  78.8 0.2 concatenate.144
  79.1 2.7 %collective-permute-start.6 = (f32[23,1,4,128]{3,0,2,1:T(8,128)S(1)}, f32[23,1,4,128]{3,0,2,1:T(8,128)S(1)}, u32[]{:S(2)}, u32[]{:S(2)}) collective-permute-start(f32[23,1,4,128]{3,0,2,1:T(8,128)S(1)} %get-tuple-element.58), channel_id=1, source_target_pairs={{0,256},{256,512},{512,768},{1,257},{257,513},{513,769},{2,258},{2... | collective-permute-start | bytes 141320 | tf_op jit(solution)/shard_map/ppermute | solution.py:28
  81.8 2.6 %collective-permute-start.7 = (f32[23,1,4,128]{3,0,2,1:T(8,128)S(1)}, f32[23,1,4,128]{3,0,2,1:T(8,128)S(1)}, u32[]{:S(2)}, u32[]{:S(2)}) collective-permute-start(f32[23,1,4,128]{3,0,2,1:T(8,128)S(1)} %get-tuple-element.57), channel_id=1, source_target_pairs={{256,0},{512,256},{768,512},{257,1},{513,257},{769,513},{258,2},{5... | collective-permute-start | bytes 141320 | tf_op jit(solution)/shard_map/ppermute | solution.py:30
  84.4 0.6 pad_subtract_fusion
  85.0 1.6 %collective-permute-done.7 = f32[23,1,4,128]{3,0,2,1:T(8,128)S(1)} collective-permute-done((f32[23,1,4,128]{3,0,2,1:T(8,128)S(1)}, f32[23,1,4,128]{3,0,2,1:T(8,128)S(1)}, u32[]{:S(2)}, u32[]{:S(2)}) %collective-permute-start.7) | collective-permute-done | bytes 47136 | tf_op jit(solution)/shard_map/ppermute | solution.py:30
  86.7 0.1 copy.121
  86.9 0.3 fusion.92
  87.2 1.9 %collective-permute-start.9 = (f32[23,10,4,1]{3,2,1,0:T(4,128)S(1)}, f32[23,10,4,1]{3,2,1,0:T(4,128)S(1)}, u32[]{:S(2)}, u32[]{:S(2)}) collective-permute-start(f32[23,10,4,1]{3,2,1,0:T(4,128)S(1)} %get-tuple-element.56), channel_id=1, source_target_pairs={{32,0},{64,32},{96,64},{128,96},{160,128},{192,160},{224,192},{33,... | collective-permute-start | bytes 11048 | tf_op jit(solution)/shard_map/ppermute | solution.py:30
  89.1 5.3 %collective-permute-start.8 = (f32[23,10,4,1]{3,2,1,0:T(4,128)S(1)}, f32[23,10,4,1]{3,2,1,0:T(4,128)S(1)}, u32[]{:S(2)}, u32[]{:S(2)}) collective-permute-start(f32[23,10,4,1]{3,2,1,0:T(4,128)S(1)} %get-tuple-element.55), channel_id=1, source_target_pairs={{0,32},{32,64},{64,96},{96,128},{128,160},{160,192},{192,224},{1,3... | collective-permute-start | bytes 11048 | tf_op jit(solution)/shard_map/ppermute | solution.py:28
  94.5 7.3 %collective-permute-done.9 = f32[23,10,4,1]{3,2,1,0:T(4,128)S(1)} collective-permute-done((f32[23,10,4,1]{3,2,1,0:T(4,128)S(1)}, f32[23,10,4,1]{3,2,1,0:T(4,128)S(1)}, u32[]{:S(2)}, u32[]{:S(2)}) %collective-permute-start.9) | collective-permute-done | bytes 3712 | tf_op jit(solution)/shard_map/ppermute | solution.py:30
  101.8 0.9 collective-permute-done.8
  102.7 1.5 %pad_maximum_fusion.41 = (f32[23,10,1,130]{3,2,1,0:T(1,128)S(1)}, f32[23,10,1,130]{3,2,1,0:T(1,128)S(1)}) fusion(f32[23,10,4,1]{3,2,1,0:T(4,128)S(1)} %collective-permute-done.9, f32[23,10,4,128]{3,2,1,0:T(4,128)S(1)} %copy.121, f32[23,10,4,1]{3,2,1,0:T(4,128)S(1)} %collective-permute-done.8), kind=kLoop, calls=%fused_computation.73 | loop fusion | flops 119600 | bytes 717600 | tf_op jit(solution)/shard_map/slice | solution.py:25
  104.2 11.7 %collective-permute-start.10 = (f32[23,10,1,130]{3,2,1,0:T(1,128)S(1)}, f32[23,10,1,130]{3,2,1,0:T(1,128)S(1)}, u32[]{:S(2)}, u32[]{:S(2)}) collective-permute-start(f32[23,10,1,130]{3,2,1,0:T(1,128)S(1)} %get-tuple-element.51), channel_id=1, source_target_pairs={{0,1},{1,2},{2,3},{3,4},{4,5},{5,6},{6,7},{7,8},{8,9},{9,10},{10,1... | collective-permute-start | bytes 358808 | tf_op jit(solution)/shard_map/ppermute | solution.py:28
  115.9 1.9 %collective-permute-start.11 = (f32[23,10,1,130]{3,2,1,0:T(1,128)S(1)}, f32[23,10,1,130]{3,2,1,0:T(1,128)S(1)}, u32[]{:S(2)}, u32[]{:S(2)}) collective-permute-start(f32[23,10,1,130]{3,2,1,0:T(1,128)S(1)} %get-tuple-element.52), channel_id=1, source_target_pairs={{1,0},{2,1},{3,2},{4,3},{5,4},{6,5},{7,6},{8,7},{9,8},{10,9},{11,1... | collective-permute-start | bytes 358808 | tf_op jit(solution)/shard_map/ppermute | solution.py:30
  117.8 0.1 maximum_bitcast_fusion.2
  118.1 0.1 copy.125
  118.2 0.1 copy.124
  118.3 0.4 subtract_multiply_fusion
  118.7 2.8 %collective-permute-done.10 = f32[23,10,1,130]{3,2,1,0:T(1,128)S(1)} collective-permute-done((f32[23,10,1,130]{3,2,1,0:T(1,128)S(1)}, f32[23,10,1,130]{3,2,1,0:T(1,128)S(1)}, u32[]{:S(2)}, u32[]{:S(2)}) %collective-permute-start.10) | collective-permute-done | bytes 119632 | tf_op jit(solution)/shard_map/ppermute | solution.py:28
  121.5 10.4 %collective-permute-done.11 = f32[23,10,1,130]{3,2,1,0:T(1,128)S(1)} collective-permute-done((f32[23,10,1,130]{3,2,1,0:T(1,128)S(1)}, f32[23,10,1,130]{3,2,1,0:T(1,128)S(1)}, u32[]{:S(2)}, u32[]{:S(2)}) %collective-permute-start.11) | collective-permute-done | bytes 119632 | tf_op jit(solution)/shard_map/ppermute | solution.py:30
  131.9 0.1 maximum_bitcast_fusion
  132.0 0.7 fusion.86
  132.8 0.5 fusion.7
  133.2 0.7 fusion.6
  133.9 0.8 copy.132
  (69 shorter events, 1.1 us)
Async XLA Ops:
  0.6 60.7 %copy-start = (f32[19,19]{1,0:T(8,128)S(1)}, f32[19,19]{1,0:T(8,128)}, u32[]{:S(2)}) copy-start(f32[19,19]{1,0:T(8,128)} %param.20) | copy-start | bytes 4336
  0.6 7.4 %copy-start.1 = (f32[19,8,4,128]{3,2,1,0:T(4,128)S(1)}, f32[19,8,4,128]{3,2,1,0:T(4,128)}, u32[]{:S(2)}) copy-start(f32[19,8,4,128]{3,2,1,0:T(4,128)} %param.17) | copy-start | bytes 933892
  2.8 7.3 %all-to-all-start = ((f32[8,4,128]{2,0,1:T(8,128)}), f32[8,4,128]{2,0,1:T(8,128)S(1)}, u32[]{:S(2)}, u32[]{:S(2)}) async-start(f32[8,4,128]{2,0,1:T(8,128)} %bitcast.254), calls=%async_computation | async-start | bytes 32768 | tf_op jit(solution)/shard_map/all_to_all | solution.py:175
  7.3 0.7 copy-start.7
  10.1 0.7 copy-start.2
  10.1 0.7 copy-start.6
  10.8 0.7 copy-start.3
  11.5 0.7 copy-start.4
  11.5 0.7 copy-start.5
  13.1 7.8 %all-to-all-start.1 = ((f32[5,32,1,128]{3,2,0,1:T(1,128)}), f32[5,32,1,128]{3,2,0,1:T(1,128)S(1)}, u32[]{:S(2)}, u32[]{:S(2)}) async-start(f32[5,32,1,128]{3,2,0,1:T(1,128)} %copy.100), calls=%async_computation.1 | async-start | bytes 163840 | tf_op jit(solution)/shard_map/all_to_all | solution.py:198
  21.2 5.4 %collective-permute-start = (f32[23,1,4,128]{3,0,2,1:T(8,128)S(1)}, f32[23,1,4,128]{3,0,2,1:T(8,128)S(1)}, u32[]{:S(2)}, u32[]{:S(2)}) collective-permute-start(f32[23,1,4,128]{3,0,2,1:T(8,128)S(1)} %get-tuple-element.60), channel_id=1, source_target_pairs={{0,256},{256,512},{512,768},{1,257},{257,513},{513,769},{2,258},{2... | collective-permute-start | bytes 141320 | tf_op jit(solution)/shard_map/ppermute | solution.py:28
  23.8 4.8 %collective-permute-start.1 = (f32[23,1,4,128]{3,0,2,1:T(8,128)S(1)}, f32[23,1,4,128]{3,0,2,1:T(8,128)S(1)}, u32[]{:S(2)}, u32[]{:S(2)}) collective-permute-start(f32[23,1,4,128]{3,0,2,1:T(8,128)S(1)} %get-tuple-element.59), channel_id=1, source_target_pairs={{256,0},{512,256},{768,512},{257,1},{513,257},{769,513},{258,2},{5... | collective-permute-start | bytes 141320 | tf_op jit(solution)/shard_map/ppermute | solution.py:30
  28.8 13.3 %collective-permute-start.3 = (f32[23,10,4,1]{3,0,2,1:T(8,128)S(1)}, f32[23,10,4,1]{3,0,2,1:T(8,128)S(1)}, u32[]{:S(2)}, u32[]{:S(2)}) collective-permute-start(f32[23,10,4,1]{3,0,2,1:T(8,128)S(1)} %get-tuple-element.54), channel_id=1, source_target_pairs={{32,0},{64,32},{96,64},{128,96},{160,128},{192,160},{224,192},{33,... | collective-permute-start | bytes 11048 | tf_op jit(solution)/shard_map/ppermute | solution.py:30
  30.8 12.3 %collective-permute-start.2 = (f32[23,10,4,1]{3,0,2,1:T(8,128)S(1)}, f32[23,10,4,1]{3,0,2,1:T(8,128)S(1)}, u32[]{:S(2)}, u32[]{:S(2)}) collective-permute-start(f32[23,10,4,1]{3,0,2,1:T(8,128)S(1)} %get-tuple-element.53), channel_id=1, source_target_pairs={{0,32},{32,64},{64,96},{96,128},{128,160},{160,192},{192,224},{1,3... | collective-permute-start | bytes 11048 | tf_op jit(solution)/shard_map/ppermute | solution.py:28
  43.3 16.2 %collective-permute-start.5 = (f32[23,10,1,130]{3,0,2,1:T(8,128)S(1)}, f32[23,10,1,130]{3,0,2,1:T(8,128)S(1)}, u32[]{:S(2)}, u32[]{:S(2)}) collective-permute-start(f32[23,10,1,130]{3,0,2,1:T(8,128)S(1)} %get-tuple-element.48), channel_id=1, source_target_pairs={{1,0},{2,1},{3,2},{4,3},{5,4},{6,5},{7,6},{8,7},{9,8},{10,9},{11,1... | collective-permute-start | bytes 358808 | tf_op jit(solution)/shard_map/ppermute | solution.py:30
  50.5 10.2 %collective-permute-start.4 = (f32[23,10,1,130]{3,0,2,1:T(8,128)S(1)}, f32[23,10,1,130]{3,0,2,1:T(8,128)S(1)}, u32[]{:S(2)}, u32[]{:S(2)}) collective-permute-start(f32[23,10,1,130]{3,0,2,1:T(8,128)S(1)} %get-tuple-element.47), channel_id=1, source_target_pairs={{0,1},{1,2},{2,3},{3,4},{4,5},{5,6},{6,7},{7,8},{8,9},{9,10},{10,1... | collective-permute-start | bytes 358808 | tf_op jit(solution)/shard_map/ppermute | solution.py:28
  61.3 0.7 copy-start.9
  61.3 0.7 copy-start.10
  61.9 0.9 copy-start.8
  79.1 6.0 %collective-permute-start.6 = (f32[23,1,4,128]{3,0,2,1:T(8,128)S(1)}, f32[23,1,4,128]{3,0,2,1:T(8,128)S(1)}, u32[]{:S(2)}, u32[]{:S(2)}) collective-permute-start(f32[23,1,4,128]{3,0,2,1:T(8,128)S(1)} %get-tuple-element.58), channel_id=1, source_target_pairs={{0,256},{256,512},{512,768},{1,257},{257,513},{513,769},{2,258},{2... | collective-permute-start | bytes 141320 | tf_op jit(solution)/shard_map/ppermute | solution.py:28
  81.8 4.8 %collective-permute-start.7 = (f32[23,1,4,128]{3,0,2,1:T(8,128)S(1)}, f32[23,1,4,128]{3,0,2,1:T(8,128)S(1)}, u32[]{:S(2)}, u32[]{:S(2)}) collective-permute-start(f32[23,1,4,128]{3,0,2,1:T(8,128)S(1)} %get-tuple-element.57), channel_id=1, source_target_pairs={{256,0},{512,256},{768,512},{257,1},{513,257},{769,513},{258,2},{5... | collective-permute-start | bytes 141320 | tf_op jit(solution)/shard_map/ppermute | solution.py:30
  87.2 14.6 %collective-permute-start.9 = (f32[23,10,4,1]{3,2,1,0:T(4,128)S(1)}, f32[23,10,4,1]{3,2,1,0:T(4,128)S(1)}, u32[]{:S(2)}, u32[]{:S(2)}) collective-permute-start(f32[23,10,4,1]{3,2,1,0:T(4,128)S(1)} %get-tuple-element.56), channel_id=1, source_target_pairs={{32,0},{64,32},{96,64},{128,96},{160,128},{192,160},{224,192},{33,... | collective-permute-start | bytes 11048 | tf_op jit(solution)/shard_map/ppermute | solution.py:30
  89.1 13.6 %collective-permute-start.8 = (f32[23,10,4,1]{3,2,1,0:T(4,128)S(1)}, f32[23,10,4,1]{3,2,1,0:T(4,128)S(1)}, u32[]{:S(2)}, u32[]{:S(2)}) collective-permute-start(f32[23,10,4,1]{3,2,1,0:T(4,128)S(1)} %get-tuple-element.55), channel_id=1, source_target_pairs={{0,32},{32,64},{64,96},{96,128},{128,160},{160,192},{192,224},{1,3... | collective-permute-start | bytes 11048 | tf_op jit(solution)/shard_map/ppermute | solution.py:28
  104.2 17.2 %collective-permute-start.10 = (f32[23,10,1,130]{3,2,1,0:T(1,128)S(1)}, f32[23,10,1,130]{3,2,1,0:T(1,128)S(1)}, u32[]{:S(2)}, u32[]{:S(2)}) collective-permute-start(f32[23,10,1,130]{3,2,1,0:T(1,128)S(1)} %get-tuple-element.51), channel_id=1, source_target_pairs={{0,1},{1,2},{2,3},{3,4},{4,5},{5,6},{6,7},{7,8},{8,9},{9,10},{10,1... | collective-permute-start | bytes 358808 | tf_op jit(solution)/shard_map/ppermute | solution.py:28
  115.9 15.9 %collective-permute-start.11 = (f32[23,10,1,130]{3,2,1,0:T(1,128)S(1)}, f32[23,10,1,130]{3,2,1,0:T(1,128)S(1)}, u32[]{:S(2)}, u32[]{:S(2)}) collective-permute-start(f32[23,10,1,130]{3,2,1,0:T(1,128)S(1)} %get-tuple-element.52), channel_id=1, source_target_pairs={{1,0},{2,1},{3,2},{4,3},{5,4},{6,5},{7,6},{8,7},{9,8},{10,9},{11,1... | collective-permute-start | bytes 358808 | tf_op jit(solution)/shard_map/ppermute | solution.py:30
where the time goes:
time: 136 us; the launch traced here: 135 us
  starting transfers between devices  60.6 us (45%)
  waiting for transfers between devices  40.5 us (30%)
  blocking collectives  13.5 us (10%)
  other arithmetic  8.11 us (6%)
  local copies, waits for them, and re-layouts  7.28 us (5%)
  matrix products  3.46 us (3%)
    ppermute x6, starting transfers between devices, with_halo(): lax.ppermute(tail, axis, [(i, (i + 1) % count) for i in range(ends)])  32.9 us
    ppermute x6, waiting for transfers between devices, with_halo(): lax.ppermute(head, axis, [((i + 1) % count, i) for i in range(ends)])  30.3 us
    ppermute x6, starting transfers between devices, with_halo(): lax.ppermute(head, axis, [((i + 1) % count, i) for i in range(ends)])  18.2 us
    all_to_all x1, blocking collectives, per_device(): lax.all_to_all(stacked, 'grp', split_axis=1, concat_axis=2, tiled=True)  7.62 us
    all_to_all x1, blocking collectives, per_device(): lax.all_to_all(pigment_band, 'grp', split_axis=1, concat_axis=0, tiled=True)  5.86 us
    ppermute x6, waiting for transfers between devices, with_halo(): lax.ppermute(tail, axis, [(i, (i + 1) % count) for i in range(ends)])  5.75 us
    all_to_all x1, starting transfers between devices, per_device(): lax.all_to_all(stacked, 'grp', split_axis=1, concat_axis=2, tiled=True)  5.01 us
    all_to_all x1, starting transfers between devices, per_device(): lax.all_to_all(pigment_band, 'grp', split_axis=1, concat_axis=0, tiled=True)  4.56 us
  transfers between devices with their start and end apart: 14, of which 12 were waited for; matrix products, arithmetic and copies ran while one was open for 3% of the time, Pallas kernels for 0%

commit v1 on v0

v1 whole, which is shorter than its diff:
```python
import functools

import jax
import jax.numpy as jnp
from jax import lax
from jax.experimental import pallas as pl
from jax.experimental.pallas import tpu as pltpu
from jax.sharding import PartitionSpec as P

STEPS = 2
NG = 4
NT = 19
F32 = jnp.float32
NF = 6


def roll(x, shift, axis):
    return pltpu.roll(x, shift % x.shape[axis], axis)


def kernel(
    nx, ny,
    u_hbm, v_hbm, t_hbm, s_hbm, q_hbm, c_hbm, dep_hbm, sol_hbm, a_s, ph_s, sat_s, pig_s,
    ou, ov, ot, osl, oc,
    cin, oc_in, dep, sol, cs, hs, hn, zup_s, zdn_s, zup_r, zdn_r, xe_s, xw_s, xe_r, xw_r,
    ps, pf, fs, fr, ush, uw, vsh, vsr, dpx, ops, mix, cw, ce, cu, cd,
    loc, psend, precv, fsend, frecv, esend, erecv, nsend, nrecv, hsend, hrecv, dsend, drecv,
):
    b = lax.axis_index("grp")
    ix = lax.axis_index("gx")
    iy = lax.axis_index("gy")
    east, west = lax.rem(ix + 1, nx), lax.rem(ix + nx - 1, nx)
    north, south = lax.rem(iy + 1, ny), lax.rem(iy + ny - 1, ny)
    peers = [lax.rem(b + k, NG) for k in (2, 3, 1)]

    barrier = pltpu.get_barrier_semaphore()
    for g in range(NG):
        for dev in ({"grp": g, "gy": north}, {"grp": g, "gy": south}, {"grp": g, "gx": east}, {"grp": g, "gx": west}):
            pl.semaphore_signal(barrier, inc=1, device_id=dev)
    for g in peers:
        pl.semaphore_signal(barrier, inc=1, device_id={"grp": g})

    loads = [pltpu.make_async_copy(c_hbm, cin, loc.at[0])]
    for n, ref in enumerate((u_hbm, v_hbm, t_hbm, s_hbm, q_hbm)):
        loads.append(pltpu.make_async_copy(ref, oc_in.at[n], loc.at[1 + n]))
    loads.append(pltpu.make_async_copy(dep_hbm, dep, loc.at[6]))
    loads.append(pltpu.make_async_copy(sol_hbm, sol, loc.at[7]))
    for copy in loads:
        copy.start()

    lane8 = lax.broadcasted_iota(jnp.int32, (8, 128), 1)
    lane32 = lax.broadcasted_iota(jnp.int32, (32, 128), 1)
    row32 = lax.broadcasted_iota(jnp.int32, (32, 128), 0)
    sends = []

    def send(src, dst, ssem, rsem, dev):
        copy = pltpu.make_async_remote_copy(src, dst, ssem, rsem, device_id=dev, device_id_type=pl.DeviceIdType.MESH)
        copy.start()
        sends.append(copy)

    def arrived(dst, ssem, rsem):
        pltpu.make_async_remote_copy(dst, dst, ssem, rsem, device_id={"grp": peers[0]}, device_id_type=pl.DeviceIdType.MESH).wait_recv()

    def publish(t):
        pig = jnp.zeros((32, 128), F32)
        for i in range(NT):
            pig = pig + pig_s[i] * cs[t, i]
        for r in range(NG):
            ps[t, r] = pig[8 * r : 8 * r + 8]
        pf[t, pl.ds(pl.multiple_of(b * 8, 8), 8), :] = ps[t, b]
        if t == 0:
            pl.semaphore_wait(barrier, 4 * NG + NG - 1)
        mine = pf.at[t, pl.ds(pl.multiple_of(b * 8, 8), 8), :]
        for k, g in enumerate(peers):
            send(ps.at[t, g], mine, psend.at[t, k], precv.at[t, b], {"grp": g})
        if t == 0:
            for k, dev in enumerate(({"gx": west}, {"gx": east}, {"gy": south}, {"gy": north})):
                send(dep_hbm, dpx.at[k], dsend.at[k], drecv.at[k], dev)
        send(cs.at[t, :, pl.ds(24, 8), :], hs.at[t], hsend.at[t, 0], hrecv.at[t, 0], {"gy": north})
        send(cs.at[t, :, pl.ds(0, 8), :], hn.at[t], hsend.at[t, 1], hrecv.at[t, 1], {"gy": south})
        pe = jnp.zeros((32, 128), F32)
        pw = jnp.zeros((32, 128), F32)
        for i in range(NT):
            x = cs[t, i]
            pe = jnp.where(lane32 == i, roll(x, i + 1, 1), pe)
            pw = jnp.where(lane32 == i, roll(x, i, 1) if i else x, pw)
        xe_s[t] = pe
        xw_s[t] = pw
        send(xe_s.at[t], xw_r.at[t], hsend.at[t, 2], hrecv.at[t, 2], {"gx": east})
        send(xw_s.at[t], xe_r.at[t], hsend.at[t, 3], hrecv.at[t, 3], {"gx": west})
        for i in range(NT):
            zup_s[t, i] = cs[t, i, pl.ds(7, NG, stride=8), :]
            zdn_s[t, i] = cs[t, i, pl.ds(0, NG, stride=8), :]

        @pl.when(b < NG - 1)
        def _():
            pltpu.make_async_remote_copy(zup_s.at[t], zup_r.at[t], hsend.at[t, 4], hrecv.at[t, 4], device_id={"grp": b + 1}, device_id_type=pl.DeviceIdType.MESH).start()

        @pl.when(b > 0)
        def _():
            pltpu.make_async_remote_copy(zdn_s.at[t], zdn_r.at[t], hsend.at[t, 5], hrecv.at[t, 5], device_id={"grp": b - 1}, device_id_type=pl.DeviceIdType.MESH).start()

    def local_terms(t):
        def mixing(i, _):
            acc = a_s[i, 0] * cs[t, 0]
            for j in range(1, NT):
                acc = acc + a_s[i, j] * cs[t, j]
            mix[i] = acc
            x = cs[t, i]
            cw[i] = roll(x, 1, 1)
            ce[i] = roll(x, 127, 1)
            cu[i] = roll(x, 1, 0)
            cd[i] = roll(x, 31, 0)
            return 0

        lax.fori_loop(0, NT, mixing, 0)

    def columns(t):
        for k, g in enumerate(peers):
            dst = pf.at[t, pl.ds(pl.multiple_of(g * 8, 8), 8), :]
            arrived(dst, psend.at[t, k], precv.at[t, g])
        att = 0.01 + 0.05 * pf[t]
        cum = att
        for s in (1, 2, 4, 8, 16):
            cum = cum + jnp.where(row32 >= s, roll(cum, s, 0), 0.0)
        top = sol[pl.ds(b, 1), :] * jnp.exp(att - cum)
        heating = top * (1.0 - jnp.exp(-att))
        par = top * jnp.exp(-0.5 * att)
        wet = (row32 < dep[pl.ds(b, 1), :]).astype(F32)
        src = oc_in if t == 0 else None
        if t == 0:
            u, v, temp, sal = (oc_in[n] for n in range(4))
        else:
            u, v, temp, sal = ou[...], ov[...], ot[...], osl[...]
        quiet = oc_in[4]
        temp = temp + 5.0 * heating * wet
        rho = 0.8 * sal - 0.2 * temp
        strat = roll(rho, 31, 0) - rho
        face = (0.5 * (quiet + roll(quiet, 31, 0)) + 0.15 * jax.nn.sigmoid(-strat)) * roll(wet, 31, 0)
        face = jnp.where(row32 < 31, face, 0.0)

        def stir(x):
            flux = face * (roll(x, 31, 0) - x)
            return x + flux - roll(flux, 1, 0)

        u, v, temp, sal = stir(u), stir(v), stir(temp), stir(sal)
        above = roll(face, 1, 0)
        ou[...] = u
        ov[...] = v
        ot[...] = temp
        osl[...] = sal
        warm = jnp.exp(0.0633 * (temp - 20.0))
        for n, x in enumerate((u, v, warm, face, above, par)):
            for g in range(NG):
                fs[t, g, n] = x[8 * g : 8 * g + 8]
        fr[t, b] = fs[t, b]
        ush[t] = roll(u, 1, 1)
        vsh[t] = v
        for k, g in enumerate(peers):
            send(fs.at[t, g], fr.at[t, b], fsend.at[t, k], frecv.at[t, b], {"grp": g})

        @pl.when(b == NG - 1)
        def _():
            for g in range(NG):
                pltpu.make_async_remote_copy(vsh.at[t, pl.ds(8 * g, 8), :], vsr.at[t], nsend.at[t, g], nrecv.at[t], device_id={"grp": g, "gy": north}, device_id_type=pl.DeviceIdType.MESH).start()

        for g in range(NG):
            send(ush.at[t, pl.ds(8 * g, 8), :], uw.at[t, b], esend.at[t, g], erecv.at[t, b], {"grp": g, "gx": east})

    def openings():
        for k in range(4):
            arrived(dpx.at[k], dsend.at[k], drecv.at[k])
        level = (lax.broadcasted_iota(jnp.int32, (8, 128), 0) + 8 * b).astype(F32)

        def wet_of(rows):
            return jnp.where(level < jnp.broadcast_to(rows, (8, 128)), 1.0, 0.0)

        def row(ref, r):
            return jnp.broadcast_to(ref[r : r + 1, :].astype(F32), (8, 128))

        own = [row(dep, r) for r in range(NG)]
        wets = [wet_of(x) for x in own]
        inside_e = (ix < nx - 1).astype(F32)
        inside_w = (ix > 0).astype(F32)
        inside_n = (iy < ny - 1).astype(F32)
        inside_s = (iy > 0).astype(F32)
        wet_n = wet_of(row(dpx.at[2], 0)) * inside_n
        wet_s = wet_of(row(dpx.at[3], NG - 1)) * inside_s
        for r in range(NG):
            wet_e = jnp.where(lane8 == 127, roll(wet_of(row(dpx.at[0], r)), 127, 1) * inside_e, roll(wets[r], 127, 1))
            wet_w = jnp.where(lane8 == 0, roll(wet_of(row(dpx.at[1], r)), 1, 1) * inside_w, roll(wets[r], 1, 1))
            ops[0, r] = wets[r] * wet_e
            ops[1, r] = wets[r] * wet_w
            ops[2, r] = wets[r] * (wets[r + 1] if r < NG - 1 else wet_n)
            ops[3, r] = wets[r] * (wets[r - 1] if r > 0 else wet_s)
            ops[4, r] = 0.5 * wets[r]

    def halos(t):
        arrived(hs.at[t], hsend.at[t, 0], hrecv.at[t, 0])
        arrived(hn.at[t], hsend.at[t, 1], hrecv.at[t, 1])
        arrived(xw_r.at[t], hsend.at[t, 2], hrecv.at[t, 2])
        arrived(xe_r.at[t], hsend.at[t, 3], hrecv.at[t, 3])
        pw = xw_r[t]
        pe = xe_r[t]
        for i in range(NT):
            cw[i] = jnp.where(lane32 == 0, roll(pw, 128 - i, 1) if i else pw, cw[i])
            ce[i] = jnp.where(lane32 == 127, roll(pe, 127 - i, 1), ce[i])

        @pl.when(b > 0)
        def _():
            arrived(zup_r.at[t], hsend.at[t, 4], hrecv.at[t, 4])
            for i in range(NT):
                cu[i, pl.ds(0, NG, stride=8), :] = zup_r[t, i]

        @pl.when(b < NG - 1)
        def _():
            arrived(zdn_r.at[t], hsend.at[t, 5], hrecv.at[t, 5])
            for i in range(NT):
                cd[i, pl.ds(7, NG, stride=8), :] = zdn_r[t, i]

    def update(t):
        for k, g in enumerate(peers):
            arrived(fr.at[t, g], fsend.at[t, k], frecv.at[t, g])
        for g in range(NG):
            arrived(uw.at[t, g], esend.at[t, g], erecv.at[t, g])
        arrived(vsr.at[t], nsend.at[t, 0], nrecv.at[t])
        for r in range(NG):
            u, v, warm, d, dm, par = (fr[t, r, n] for n in range(NF))
            uwest = jnp.where(lane8 == 0, uw[t, r], roll(u, 1, 1))
            vsouth = fr[t, r - 1, 1] if r > 0 else vsr[t]
            a_e = ops[0, r] * (jnp.maximum(u, 0.0) + 0.05)
            b_e = ops[0, r] * (0.05 - jnp.minimum(u, 0.0))
            a_w = ops[1, r] * (jnp.maximum(uwest, 0.0) + 0.05)
            b_w = ops[1, r] * (0.05 - jnp.minimum(uwest, 0.0))
            a_n = ops[2, r] * (jnp.maximum(v, 0.0) + 0.05)
            b_n = ops[2, r] * (0.05 - jnp.minimum(v, 0.0))
            a_s_ = ops[3, r] * (jnp.maximum(vsouth, 0.0) + 0.05)
            b_s = ops[3, r] * (0.05 - jnp.minimum(vsouth, 0.0))
            k0 = 1.0 - a_e - b_w - a_n - b_s - d - dm
            half = ops[4, r]
            warm = half * warm
            parw = half * par
            rows = pl.ds(8 * r, 8)

            def one(i, _):
                x = cs[t, i, rows, :]
                up = cs[t, i, pl.ds(8 * r + 8, 8), :] if r < NG - 1 else hn[t, i]
                dn = cs[t, i, pl.ds(8 * r - 8, 8), :] if r > 0 else hs[t, i]
                grow = k0 + ph_s[i] * parw / (par + sat_s[i])
                new = (
                    grow * x
                    + (b_e * ce[i, rows, :] + a_w * cw[i, rows, :])
                    + (b_n * up + a_s_ * dn)
                    + (d * cd[i, rows, :] + dm * cu[i, rows, :])
                    + warm * mix[i, rows, :]
                )
                if t == STEPS - 1:
                    oc[pl.ds(i * 32 + r, 8, stride=4), :] = new
                else:
                    cs[t + 1, i, rows, :] = new
                return 0

            lax.fori_loop(0, NT, one, 0, unroll=True)

    loads[0].wait()
    for i in range(NT):
        for r in range(NG):
            cs[0, i, pl.ds(8 * r, 8), :] = cin[pl.ds(i * 32 + r, 8, stride=4), :]
    loads[6].wait()
    publish(0)
    for copy in loads[1:6] + loads[7:]:
        copy.wait()
    local_terms(0)
    openings()
    columns(0)
    halos(0)
    update(0)
    publish(1)
    local_terms(1)
    columns(1)
    halos(1)
    update(1)

    for copy in sends:
        copy.wait_send()
    for t in range(STEPS):

        @pl.when(b < NG - 1)
        def _():
            pltpu.make_async_remote_copy(zup_s.at[t], zup_r.at[t], hsend.at[t, 4], hrecv.at[t, 4], device_id={"grp": b + 1}, device_id_type=pl.DeviceIdType.MESH).wait_send()

        @pl.when(b > 0)
        def _():
            pltpu.make_async_remote_copy(zdn_s.at[t], zdn_r.at[t], hsend.at[t, 5], hrecv.at[t, 5], device_id={"grp": b - 1}, device_id_type=pl.DeviceIdType.MESH).wait_send()

        @pl.when(b == NG - 1)
        def _():
            for g in range(NG):
                pltpu.make_async_remote_copy(vsh.at[t, pl.ds(8 * g, 8), :], vsr.at[t], nsend.at[t, g], nrecv.at[t], device_id={"grp": g, "gy": north}, device_id_type=pl.DeviceIdType.MESH).wait_send()


def per_device(nx, ny, *args):
    u, v, temp, sal, quiet, c, dep, sol, rates, photo, satur, pig = args
    shape = u.shape
    fields = [x.reshape(32, 128) for x in (u, v, temp, sal, quiet)]
    hbm = pl.BlockSpec(memory_space=pl.ANY)
    smem = pl.BlockSpec(memory_space=pltpu.SMEM)
    vmem = pl.BlockSpec(memory_space=pltpu.VMEM)
    col = jax.ShapeDtypeStruct((32, 128), F32)
    V = pltpu.VMEM
    D = pltpu.SemaphoreType.DMA
    S = STEPS
    out = pl.pallas_call(
        functools.partial(kernel, nx, ny),
        out_shape=(col, col, col, col, jax.ShapeDtypeStruct((NT * 32, 128), F32)),
        in_specs=[hbm] * 8 + [smem] * 4,
        out_specs=(vmem,) * 5,
        scratch_shapes=[
            V((NT * 32, 128), F32), V((5, 32, 128), F32), V((4, 128), jnp.int32), V((4, 128), F32),
            V((S, NT, 32, 128), F32), V((S, NT, 8, 128), F32), V((S, NT, 8, 128), F32),
            V((S, NT, 4, 128), F32), V((S, NT, 4, 128), F32), V((S, NT, 4, 128), F32), V((S, NT, 4, 128), F32),
            V((S, 32, 128), F32), V((S, 32, 128), F32), V((S, 32, 128), F32), V((S, 32, 128), F32),
            V((S, NG, 8, 128), F32), V((S, 32, 128), F32),
            V((S, NG, NF, 8, 128), F32), V((S, NG, NF, 8, 128), F32),
            V((S, 32, 128), F32), V((S, NG, 8, 128), F32), V((S, 32, 128), F32), V((S, 8, 128), F32),
            V((4, 4, 128), jnp.int32), V((5, NG, 8, 128), F32),
            V((NT, 32, 128), F32), V((NT, 32, 128), F32), V((NT, 32, 128), F32), V((NT, 32, 128), F32), V((NT, 32, 128), F32),
            D((8,)), D((S, 3)), D((S, NG)), D((S, 3)), D((S, NG)), D((S, NG)), D((S, NG)), D((S, NG)), D((S,)),
            D((S, 6)), D((S, 6)), D((4,)), D((4,)),
        ],
        compiler_params=pltpu.CompilerParams(collective_id=0, has_side_effects=True),
    )(*fields, c.reshape(NT * 32, 128), dep, sol, rates, photo, satur, pig)
    return tuple(x.reshape(shape) for x in out[:4]) + (out[4].reshape(c.shape),)


def solution(mesh):
    field = P(None, "gy", "grp", "gx")
    tracer = P(None, "grp", "gy", "gx")
    flat = P("gy", "gx")
    return jax.shard_map(
        functools.partial(per_device, mesh.shape["gx"], mesh.shape["gy"]),
        mesh=mesh,
        in_specs=(field,) * 5 + (tracer, flat, flat, P(), P(), P(), P()),
        out_specs=(field,) * 4 + (tracer,),
        check_vma=False,
    )
```

time: 136 us -> 52.1 us (0.38)
  the two profiles are of different devices: /device:TPU:501 before, /device:TPU:14 now
where the time goes in v1:
time: 52.1 us; the launch traced here: 51.6 us
  Pallas kernels  45.7 us (88%)
  local copies, waits for them, and re-layouts  5.19 us (10%)
  between operations  0.66 us (1%)
    pallas_call x1, Pallas kernels, per_device(): pl.pallas_call(functools.partial(kernel, nx, ny), out_shape=(col, col, co...  45.7 us
    unnamed x13, local copies, waits for them, and re-layouts  5.19 us

profile of v1, /device:TPU:14, one launch (start us, length us, event | category | flops | bytes accessed | tf_op | source)
XLA Modules:
  0.0 51.6 jit_solution(10165423103145235856)
XLA Ops:
  0.6 45.7 %shard_map.155 = (f32[32,128]{1,0:T(8,128)}, f32[32,128]{1,0:T(8,128)}, f32[32,128]{1,0:T(8,128)}, f32[32,128]{1,0:T(8,128)}, f32[608,128]{1,0:T(8,128)}) custom-call(f32[32,128]{1,0:T(8,128)} %bitcast.21, f32[32,128]{1,0:T(8,128)} %bitcast.22, f32[32,128]{1,0:T(8,128)} %bitcast.23, f32[32,128]{1,0:T(8,128)} %bitcast.24, f32[32,128]{1,0:T(8,128)} %bitcast.25, ...), custom_call_target="tpu_custom_call" | custom-call | tf_op jit(solution)/shard_map/pallas_call | solution.py:313
  46.4 0.0 copy-start.3
  46.4 0.7 %copy-done.3 = f32[32,128]{1,0:T(8,128)S(1)} copy-done((f32[32,128]{1,0:T(8,128)S(1)}, f32[32,128]{1,0:T(8,128)}, u32[]{:S(2)}) %copy-start.3) | copy-done | bytes 16408
  47.1 0.0 copy-start.2
  47.1 0.6 %copy.26 = f32[32,1,1,128]{3,2,1,0:T(1,128)} copy(f32[32,1,1,128]{3,2,1,0:T(1,128)S(1)} %bitcast.29) | data formatting | bytes 32768
  47.7 0.1 copy-done.2
  47.8 0.0 copy-start.1
  47.8 0.6 %copy.27 = f32[32,1,1,128]{3,2,1,0:T(1,128)} copy(f32[32,1,1,128]{3,2,1,0:T(1,128)S(1)} %bitcast.28) | data formatting | bytes 32768
  48.4 0.1 copy-done.1
  48.5 0.0 copy-start
  48.5 0.6 %copy.28 = f32[32,1,1,128]{3,2,1,0:T(1,128)} copy(f32[32,1,1,128]{3,2,1,0:T(1,128)S(1)} %bitcast.27) | data formatting | bytes 32768
  49.1 0.1 copy-done
  49.2 0.6 %copy.29 = f32[32,1,1,128]{3,2,1,0:T(1,128)} copy(f32[32,1,1,128]{3,2,1,0:T(1,128)S(1)} %bitcast.26) | data formatting | bytes 32768
  49.9 1.7 %copy.30 = f32[19,8,4,128]{3,2,1,0:T(4,128)} copy(f32[19,8,4,128]{3,2,1,0:T(4,128)} %bitcast.20) | data formatting | bytes 622592
Async XLA Ops:
  46.4 0.7 %copy-start.3 = (f32[32,128]{1,0:T(8,128)S(1)}, f32[32,128]{1,0:T(8,128)}, u32[]{:S(2)}) copy-start(f32[32,128]{1,0:T(8,128)} %get-tuple-element.10) | copy-start | bytes 49156
  47.1 0.7 %copy-start.2 = (f32[32,128]{1,0:T(8,128)S(1)}, f32[32,128]{1,0:T(8,128)}, u32[]{:S(2)}) copy-start(f32[32,128]{1,0:T(8,128)} %get-tuple-element.11) | copy-start | bytes 49156
  47.8 0.7 %copy-start.1 = (f32[32,128]{1,0:T(8,128)S(1)}, f32[32,128]{1,0:T(8,128)}, u32[]{:S(2)}) copy-start(f32[32,128]{1,0:T(8,128)} %get-tuple-element.12) | copy-start | bytes 49156
  48.5 0.7 %copy-start = (f32[32,128]{1,0:T(8,128)S(1)}, f32[32,128]{1,0:T(8,128)}, u32[]{:S(2)}) copy-start(f32[32,128]{1,0:T(8,128)} %get-tuple-element.13) | copy-start | bytes 49156

commit v2 on v1

--- a/solution.py
+++ b/solution.py
@@ -29,14 +29,19 @@
     b = lax.axis_index("grp")
     ix = lax.axis_index("gx")
     iy = lax.axis_index("gy")
-    east, west = lax.rem(ix + 1, nx), lax.rem(ix + nx - 1, nx)
-    north, south = lax.rem(iy + 1, ny), lax.rem(iy + ny - 1, ny)
+    has_e, has_w, has_n, has_s = ix < nx - 1, ix > 0, iy < ny - 1, iy > 0
+    east, west, north, south = {"gx": ix + 1}, {"gx": ix - 1}, {"gy": iy + 1}, {"gy": iy - 1}
+    sides = ((has_w, west), (has_e, east), (has_s, south), (has_n, north))
     peers = [lax.rem(b + k, NG) for k in (2, 3, 1)]
 
     barrier = pltpu.get_barrier_semaphore()
-    for g in range(NG):
-        for dev in ({"grp": g, "gy": north}, {"grp": g, "gy": south}, {"grp": g, "gx": east}, {"grp": g, "gx": west}):
-            pl.semaphore_signal(barrier, inc=1, device_id=dev)
+    for there, dev in sides:
+
+        @pl.when(there)
+        def _():
+            for g in range(NG):
+                pl.semaphore_signal(barrier, inc=1, device_id={"grp": g, **dev})
+
     for g in peers:
         pl.semaphore_signal(barrier, inc=1, device_id={"grp": g})
 
@@ -53,13 +58,33 @@
     row32 = lax.broadcasted_iota(jnp.int32, (32, 128), 0)
     sends = []
 
-    def send(src, dst, ssem, rsem, dev):
+    def send(src, dst, ssem, rsem, dev, there=None):
         copy = pltpu.make_async_remote_copy(src, dst, ssem, rsem, device_id=dev, device_id_type=pl.DeviceIdType.MESH)
-        copy.start()
-        sends.append(copy)
-
-    def arrived(dst, ssem, rsem):
-        pltpu.make_async_remote_copy(dst, dst, ssem, rsem, device_id={"grp": peers[0]}, device_id_type=pl.DeviceIdType.MESH).wait_recv()
+        sends.append((there, copy))
+        if there is None:
+            copy.start()
+        else:
+            pl.when(there)(copy.start)
+
+    def arrived(dst, ssem, rsem, there=None):
+        copy = pltpu.make_async_remote_copy(dst, dst, ssem, rsem, device_id={"grp": peers[0]}, device_id_type=pl.DeviceIdType.MESH)
+        if there is None:
+            copy.wait_recv()
+        else:
+            pl.when(there)(copy.wait_recv)
+
+    for there, refs in ((has_w, (uw, xw_r)), (has_e, (xe_r,)), (has_s, (vsr, hs)), (has_n, (hn,))):
+
+        @pl.when(jnp.logical_not(there))
+        def _():
+            for ref in refs:
+                ref[...] = jnp.zeros_like(ref)
+
+    for k, (there, _) in enumerate(sides):
+
+        @pl.when(jnp.logical_not(there))
+        def _():
+            dpx[k] = jnp.zeros((4, 128), jnp.int32)
 
     def publish(t):
         pig = jnp.zeros((32, 128), F32)
@@ -69,15 +94,15 @@
             ps[t, r] = pig[8 * r : 8 * r + 8]
         pf[t, pl.ds(pl.multiple_of(b * 8, 8), 8), :] = ps[t, b]
         if t == 0:
-            pl.semaphore_wait(barrier, 4 * NG + NG - 1)
+            pl.semaphore_wait(barrier, NG - 1 + NG * sum(there.astype(jnp.int32) for there, _ in sides))
         mine = pf.at[t, pl.ds(pl.multiple_of(b * 8, 8), 8), :]
         for k, g in enumerate(peers):
             send(ps.at[t, g], mine, psend.at[t, k], precv.at[t, b], {"grp": g})
         if t == 0:
-            for k, dev in enumerate(({"gx": west}, {"gx": east}, {"gy": south}, {"gy": north})):
-                send(dep_hbm, dpx.at[k], dsend.at[k], drecv.at[k], dev)
-        send(cs.at[t, :, pl.ds(24, 8), :], hs.at[t], hsend.at[t, 0], hrecv.at[t, 0], {"gy": north})
-        send(cs.at[t, :, pl.ds(0, 8), :], hn.at[t], hsend.at[t, 1], hrecv.at[t, 1], {"gy": south})
+            for k, (there, dev) in enumerate(sides):
+                send(dep_hbm, dpx.at[k ^ 1], dsend.at[k], drecv.at[k ^ 1], dev, there)
+        send(cs.at[t, :, pl.ds(24, 8), :], hs.at[t], hsend.at[t, 0], hrecv.at[t, 0], north, has_n)
+        send(cs.at[t, :, pl.ds(0, 8), :], hn.at[t], hsend.at[t, 1], hrecv.at[t, 1], south, has_s)
         pe = jnp.zeros((32, 128), F32)
         pw = jnp.zeros((32, 128), F32)
         for i in range(NT):
@@ -86,19 +111,14 @@
             pw = jnp.where(lane32 == i, roll(x, i, 1) if i else x, pw)
         xe_s[t] = pe
         xw_s[t] = pw
-        send(xe_s.at[t], xw_r.at[t], hsend.at[t, 2], hrecv.at[t, 2], {"gx": east})
-        send(xw_s.at[t], xe_r.at[t], hsend.at[t, 3], hrecv.at[t, 3], {"gx": west})
+        send(xe_s.at[t], xw_r.at[t], hsend.at[t, 2], hrecv.at[t, 2], east, has_e)
+        send(xw_s.at[t], xe_r.at[t], hsend.at[t, 3], hrecv.at[t, 3], west, has_w)
         for i in range(NT):
             zup_s[t, i] = cs[t, i, pl.ds(7, NG, stride=8), :]
             zdn_s[t, i] = cs[t, i, pl.ds(0, NG, stride=8), :]
 
-        @pl.when(b < NG - 1)
-        def _():
-            pltpu.make_async_remote_copy(zup_s.at[t], zup_r.at[t], hsend.at[t, 4], hrecv.at[t, 4], device_id={"grp": b + 1}, device_id_type=pl.DeviceIdType.MESH).start()
-
-        @pl.when(b > 0)
-        def _():
-            pltpu.make_async_remote_copy(zdn_s.at[t], zdn_r.at[t], hsend.at[t, 5], hrecv.at[t, 5], device_id={"grp": b - 1}, device_id_type=pl.DeviceIdType.MESH).start()
+        send(zup_s.at[t], zup_r.at[t], hsend.at[t, 4], hrecv.at[t, 4], {"grp": b + 1}, b < NG - 1)
+        send(zdn_s.at[t], zdn_r.at[t], hsend.at[t, 5], hrecv.at[t, 5], {"grp": b - 1}, b > 0)
 
     def local_terms(t):
         def mixing(i, _):
@@ -127,7 +147,6 @@
         heating = top * (1.0 - jnp.exp(-att))
         par = top * jnp.exp(-0.5 * att)
         wet = (row32 < dep[pl.ds(b, 1), :]).astype(F32)
-        src = oc_in if t == 0 else None
         if t == 0:
             u, v, temp, sal = (oc_in[n] for n in range(4))
         else:
@@ -159,17 +178,13 @@
         for k, g in enumerate(peers):
             send(fs.at[t, g], fr.at[t, b], fsend.at[t, k], frecv.at[t, b], {"grp": g})
 
-        @pl.when(b == NG - 1)
-        def _():
-            for g in range(NG):
-                pltpu.make_async_remote_copy(vsh.at[t, pl.ds(8 * g, 8), :], vsr.at[t], nsend.at[t, g], nrecv.at[t], device_id={"grp": g, "gy": north}, device_id_type=pl.DeviceIdType.MESH).start()
-
         for g in range(NG):
-            send(ush.at[t, pl.ds(8 * g, 8), :], uw.at[t, b], esend.at[t, g], erecv.at[t, b], {"grp": g, "gx": east})
+            send(vsh.at[t, pl.ds(8 * g, 8), :], vsr.at[t], nsend.at[t, g], nrecv.at[t], {"grp": g, **north}, jnp.logical_and(b == NG - 1, has_n))
+            send(ush.at[t, pl.ds(8 * g, 8), :], uw.at[t, b], esend.at[t, g], erecv.at[t, b], {"grp": g, **east}, has_e)
 
     def openings():
         for k in range(4):
-            arrived(dpx.at[k], dsend.at[k], drecv.at[k])
+            arrived(dpx.at[k], dsend.at[k], drecv.at[k], sides[k][0])
         level = (lax.broadcasted_iota(jnp.int32, (8, 128), 0) + 8 * b).astype(F32)
 
         def wet_of(rows):
@@ -180,15 +195,11 @@
 
         own = [row(dep, r) for r in range(NG)]
         wets = [wet_of(x) for x in own]
-        inside_e = (ix < nx - 1).astype(F32)
-        inside_w = (ix > 0).astype(F32)
-        inside_n = (iy < ny - 1).astype(F32)
-        inside_s = (iy > 0).astype(F32)
-        wet_n = wet_of(row(dpx.at[2], 0)) * inside_n
-        wet_s = wet_of(row(dpx.at[3], NG - 1)) * inside_s
+        wet_n = wet_of(row(dpx.at[3], 0))
+        wet_s = wet_of(row(dpx.at[2], NG - 1))
         for r in range(NG):
-            wet_e = jnp.where(lane8 == 127, roll(wet_of(row(dpx.at[0], r)), 127, 1) * inside_e, roll(wets[r], 127, 1))
-            wet_w = jnp.where(lane8 == 0, roll(wet_of(row(dpx.at[1], r)), 1, 1) * inside_w, roll(wets[r], 1, 1))
+            wet_e = jnp.where(lane8 == 127, roll(wet_of(row(dpx.at[1], r)), 127, 1), roll(wets[r], 127, 1))
+            wet_w = jnp.where(lane8 == 0, roll(wet_of(row(dpx.at[0], r)), 1, 1), roll(wets[r], 1, 1))
             ops[0, r] = wets[r] * wet_e
             ops[1, r] = wets[r] * wet_w
             ops[2, r] = wets[r] * (wets[r + 1] if r < NG - 1 else wet_n)
@@ -196,10 +207,10 @@
             ops[4, r] = 0.5 * wets[r]
 
     def halos(t):
-        arrived(hs.at[t], hsend.at[t, 0], hrecv.at[t, 0])
-        arrived(hn.at[t], hsend.at[t, 1], hrecv.at[t, 1])
-        arrived(xw_r.at[t], hsend.at[t, 2], hrecv.at[t, 2])
-        arrived(xe_r.at[t], hsend.at[t, 3], hrecv.at[t, 3])
+        arrived(hs.at[t], hsend.at[t, 0], hrecv.at[t, 0], has_s)
+        arrived(hn.at[t], hsend.at[t, 1], hrecv.at[t, 1], has_n)
+        arrived(xw_r.at[t], hsend.at[t, 2], hrecv.at[t, 2], has_w)
+        arrived(xe_r.at[t], hsend.at[t, 3], hrecv.at[t, 3], has_e)
         pw = xw_r[t]
         pe = xe_r[t]
         for i in range(NT):
@@ -222,8 +233,8 @@
         for k, g in enumerate(peers):
             arrived(fr.at[t, g], fsend.at[t, k], frecv.at[t, g])
         for g in range(NG):
-            arrived(uw.at[t, g], esend.at[t, g], erecv.at[t, g])
-        arrived(vsr.at[t], nsend.at[t, 0], nrecv.at[t])
+            arrived(uw.at[t, g], esend.at[t, g], erecv.at[t, g], has_w)
+        arrived(vsr.at[t], nsend.at[t, 0], nrecv.at[t], has_s)
         for r in range(NG):
             u, v, warm, d, dm, par = (fr[t, r, n] for n in range(NF))
             uwest = jnp.where(lane8 == 0, uw[t, r], roll(u, 1, 1))
@@ -281,22 +292,11 @@
     halos(1)
     update(1)
 
-    for copy in sends:
-        copy.wait_send()
-    for t in range(STEPS):
-
-        @pl.when(b < NG - 1)
-        def _():
-            pltpu.make_async_remote_copy(zup_s.at[t], zup_r.at[t], hsend.at[t, 4], hrecv.at[t, 4], device_id={"grp": b + 1}, device_id_type=pl.DeviceIdType.MESH).wait_send()
-
-        @pl.when(b > 0)
-        def _():
-            pltpu.make_async_remote_copy(zdn_s.at[t], zdn_r.at[t], hsend.at[t, 5], hrecv.at[t, 5], device_id={"grp": b - 1}, device_id_type=pl.DeviceIdType.MESH).wait_send()
-
-        @pl.when(b == NG - 1)
-        def _():
-            for g in range(NG):
-                pltpu.make_async_remote_copy(vsh.at[t, pl.ds(8 * g, 8), :], vsr.at[t], nsend.at[t, g], nrecv.at[t], device_id={"grp": g, "gy": north}, device_id_type=pl.DeviceIdType.MESH).wait_send()
+    for there, copy in sends:
+        if there is None:
+            copy.wait_send()
+        else:
+            pl.when(there)(copy.wait_send)
 
 
 def per_device(nx, ny, *args):

time: 52.1 us -> 41.7 us (0.80)
  the two profiles are of different devices: /device:TPU:14 before, /device:TPU:1 now
where the time goes in v2:
time: 41.7 us; the launch traced here: 41.1 us
  Pallas kernels  35.3 us (85%)
  local copies, waits for them, and re-layouts  5.19 us (12%)
  between operations  0.66 us (2%)
    pallas_call x1, Pallas kernels, per_device(): pl.pallas_call(functools.partial(kernel, nx, ny), out_shape=(col, col, co...  35.3 us
    unnamed x13, local copies, waits for them, and re-layouts  5.19 us

profile of v2, /device:TPU:1, one launch (start us, length us, event | category | flops | bytes accessed | tf_op | source)
XLA Modules:
  0.0 41.1 jit_solution(8165514077952395793)
XLA Ops:
  0.6 35.3 %shard_map.155 = (f32[32,128]{1,0:T(8,128)}, f32[32,128]{1,0:T(8,128)}, f32[32,128]{1,0:T(8,128)}, f32[32,128]{1,0:T(8,128)}, f32[608,128]{1,0:T(8,128)}) custom-call(f32[32,128]{1,0:T(8,128)} %bitcast.21, f32[32,128]{1,0:T(8,128)} %bitcast.22, f32[32,128]{1,0:T(8,128)} %bitcast.23, f32[32,128]{1,0:T(8,128)} %bitcast.24, f32[32,128]{1,0:T(8,128)} %bitcast.25, ...), custom_call_target="tpu_custom_call" | custom-call | tf_op jit(solution)/shard_map/pallas_call | solution.py:313
  35.9 0.0 copy-start.3
  35.9 0.7 %copy-done.3 = f32[32,128]{1,0:T(8,128)S(1)} copy-done((f32[32,128]{1,0:T(8,128)S(1)}, f32[32,128]{1,0:T(8,128)}, u32[]{:S(2)}) %copy-start.3) | copy-done | bytes 16408
  36.6 0.0 copy-start.2
  36.6 0.6 %copy.26 = f32[32,1,1,128]{3,2,1,0:T(1,128)} copy(f32[32,1,1,128]{3,2,1,0:T(1,128)S(1)} %bitcast.29) | data formatting | bytes 32768
  37.2 0.1 copy-done.2
  37.4 0.0 copy-start.1
  37.4 0.6 %copy.27 = f32[32,1,1,128]{3,2,1,0:T(1,128)} copy(f32[32,1,1,128]{3,2,1,0:T(1,128)S(1)} %bitcast.28) | data formatting | bytes 32768
  38.0 0.1 copy-done.1
  38.1 0.0 copy-start
  38.1 0.6 %copy.28 = f32[32,1,1,128]{3,2,1,0:T(1,128)} copy(f32[32,1,1,128]{3,2,1,0:T(1,128)S(1)} %bitcast.27) | data formatting | bytes 32768
  38.7 0.1 copy-done
  38.8 0.6 %copy.29 = f32[32,1,1,128]{3,2,1,0:T(1,128)} copy(f32[32,1,1,128]{3,2,1,0:T(1,128)S(1)} %bitcast.26) | data formatting | bytes 32768
  39.4 1.7 %copy.30 = f32[19,8,4,128]{3,2,1,0:T(4,128)} copy(f32[19,8,4,128]{3,2,1,0:T(4,128)} %bitcast.20) | data formatting | bytes 622592
Async XLA Ops:
  35.9 0.7 %copy-start.3 = (f32[32,128]{1,0:T(8,128)S(1)}, f32[32,128]{1,0:T(8,128)}, u32[]{:S(2)}) copy-start(f32[32,128]{1,0:T(8,128)} %get-tuple-element.10) | copy-start | bytes 49156
  36.6 0.7 %copy-start.2 = (f32[32,128]{1,0:T(8,128)S(1)}, f32[32,128]{1,0:T(8,128)}, u32[]{:S(2)}) copy-start(f32[32,128]{1,0:T(8,128)} %get-tuple-element.11) | copy-start | bytes 49156
  37.4 0.7 %copy-start.1 = (f32[32,128]{1,0:T(8,128)S(1)}, f32[32,128]{1,0:T(8,128)}, u32[]{:S(2)}) copy-start(f32[32,128]{1,0:T(8,128)} %get-tuple-element.12) | copy-start | bytes 49156
  38.1 0.7 %copy-start = (f32[32,128]{1,0:T(8,128)S(1)}, f32[32,128]{1,0:T(8,128)}, u32[]{:S(2)}) copy-start(f32[32,128]{1,0:T(8,128)} %get-tuple-element.13) | copy-start | bytes 49156

commit v3 on v2

--- a/solution.py
+++ b/solution.py
@@ -20,9 +20,9 @@
 
 def kernel(
     nx, ny,
-    u_hbm, v_hbm, t_hbm, s_hbm, q_hbm, c_hbm, dep_hbm, sol_hbm, a_s, ph_s, sat_s, pig_s,
+    u_hbm, v_hbm, t_hbm, s_hbm, q_hbm, c_hbm, dep_hbm, sol_hbm, a_hbm, ph_hbm, sat_hbm, pig_hbm,
     ou, ov, ot, osl, oc,
-    cin, oc_in, dep, sol, cs, hs, hn, zup_s, zdn_s, zup_r, zdn_r, xe_s, xw_s, xe_r, xw_r,
+    a_s, ph_s, sat_s, pig_s, cin, oc_in, dep, sol, cs, hs, hn, zup_s, zdn_s, zup_r, zdn_r, xe_s, xw_s, xe_r, xw_r,
     ps, pf, fs, fr, ush, uw, vsh, vsr, dpx, ops, mix, cw, ce, cu, cd,
     loc, psend, precv, fsend, frecv, esend, erecv, nsend, nrecv, hsend, hrecv, dsend, drecv,
 ):
@@ -50,6 +50,8 @@
         loads.append(pltpu.make_async_copy(ref, oc_in.at[n], loc.at[1 + n]))
     loads.append(pltpu.make_async_copy(dep_hbm, dep, loc.at[6]))
     loads.append(pltpu.make_async_copy(sol_hbm, sol, loc.at[7]))
+    for n, (ref, dst) in enumerate(((pig_hbm, pig_s), (a_hbm, a_s), (ph_hbm, ph_s), (sat_hbm, sat_s))):
+        loads.append(pltpu.make_async_copy(ref, dst, loc.at[8 + n]))
     for copy in loads:
         copy.start()
 
@@ -277,9 +279,9 @@
     for i in range(NT):
         for r in range(NG):
             cs[0, i, pl.ds(8 * r, 8), :] = cin[pl.ds(i * 32 + r, 8, stride=4), :]
-    loads[6].wait()
+    loads[8].wait()
     publish(0)
-    for copy in loads[1:6] + loads[7:]:
+    for copy in loads[1:8] + loads[9:]:
         copy.wait()
     local_terms(0)
     openings()
@@ -299,12 +301,20 @@
             pl.when(there)(copy.wait_send)
 
 
+def write_out(*refs):
+    n = (len(refs) - 1) // 2
+    copies = [pltpu.make_async_copy(refs[k], refs[n + k], refs[-1].at[k]) for k in range(n)]
+    for copy in copies:
+        copy.start()
+    for copy in copies:
+        copy.wait()
+
+
 def per_device(nx, ny, *args):
     u, v, temp, sal, quiet, c, dep, sol, rates, photo, satur, pig = args
     shape = u.shape
     fields = [x.reshape(32, 128) for x in (u, v, temp, sal, quiet)]
-    hbm = pl.BlockSpec(memory_space=pl.ANY)
-    smem = pl.BlockSpec(memory_space=pltpu.SMEM)
+    hbm = pl.BlockSpec(memory_space=pltpu.HBM)
     vmem = pl.BlockSpec(memory_space=pltpu.VMEM)
     col = jax.ShapeDtypeStruct((32, 128), F32)
     V = pltpu.VMEM
@@ -313,9 +323,10 @@
     out = pl.pallas_call(
         functools.partial(kernel, nx, ny),
         out_shape=(col, col, col, col, jax.ShapeDtypeStruct((NT * 32, 128), F32)),
-        in_specs=[hbm] * 8 + [smem] * 4,
+        in_specs=[hbm] * 12,
         out_specs=(vmem,) * 5,
         scratch_shapes=[
+            pltpu.SMEM((NT, NT), F32), pltpu.SMEM((NT,), F32), pltpu.SMEM((NT,), F32), pltpu.SMEM((NT,), F32),
             V((NT * 32, 128), F32), V((5, 32, 128), F32), V((4, 128), jnp.int32), V((4, 128), F32),
             V((S, NT, 32, 128), F32), V((S, NT, 8, 128), F32), V((S, NT, 8, 128), F32),
             V((S, NT, 4, 128), F32), V((S, NT, 4, 128), F32), V((S, NT, 4, 128), F32), V((S, NT, 4, 128), F32),
@@ -325,11 +336,19 @@
             V((S, 32, 128), F32), V((S, NG, 8, 128), F32), V((S, 32, 128), F32), V((S, 8, 128), F32),
             V((4, 4, 128), jnp.int32), V((5, NG, 8, 128), F32),
             V((NT, 32, 128), F32), V((NT, 32, 128), F32), V((NT, 32, 128), F32), V((NT, 32, 128), F32), V((NT, 32, 128), F32),
-            D((8,)), D((S, 3)), D((S, NG)), D((S, 3)), D((S, NG)), D((S, NG)), D((S, NG)), D((S, NG)), D((S,)),
+            D((12,)), D((S, 3)), D((S, NG)), D((S, 3)), D((S, NG)), D((S, NG)), D((S, NG)), D((S, NG)), D((S,)),
             D((S, 6)), D((S, 6)), D((4,)), D((4,)),
         ],
-        compiler_params=pltpu.CompilerParams(collective_id=0, has_side_effects=True),
-    )(*fields, c.reshape(NT * 32, 128), dep, sol, rates, photo, satur, pig)
+        compiler_params=pltpu.CompilerParams(collective_id=0, has_side_effects=True, vmem_limit_bytes=16 << 20),
+    )(*[pltpu.with_memory_space_constraint(x, pltpu.HBM) for x in (*fields, c.reshape(NT * 32, 128), dep, sol, rates, photo, satur, pig)])
+    out = pl.pallas_call(
+        write_out,
+        out_shape=(col, col, col, col, jax.ShapeDtypeStruct((NT * 32, 128), F32)),
+        in_specs=[vmem] * 5,
+        out_specs=(hbm,) * 5,
+        scratch_shapes=[D((5,))],
+        compiler_params=pltpu.CompilerParams(vmem_limit_bytes=4 << 20),
+    )(*out)
     return tuple(x.reshape(shape) for x in out[:4]) + (out[4].reshape(c.shape),)
 
 

time: 41.7 us -> 35.3 us (0.85)
  local copies, waits for them, and re-layouts: 5.19 us -> 0 us
  Pallas kernels: 35.3 us -> 34.5 us
    unnamed x13 -> x0, local copies, waits for them, and re-layouts: 5.19 us -> none
    pallas_call x1, Pallas kernels: 35.3 us -> 33.7 us  [per_device(): pl.pallas_call(functools.partial(kernel, nx, ny), out_shape=(col, col, co...]
    pallas_call x0 -> x1, Pallas kernels: none -> 0.79 us  [per_device(): pl.pallas_call(write_out, out_shape=(col, col, col, col, jax.ShapeDtypeSt...]
where the time goes in v3:
time: 35.3 us; the launch traced here: 35.1 us
  Pallas kernels  34.5 us (98%)
  between operations  0.64 us (2%)
    pallas_call x1, Pallas kernels, per_device(): pl.pallas_call(functools.partial(kernel, nx, ny), out_shape=(col, col, co...  33.7 us
    pallas_call x1, Pallas kernels, per_device(): pl.pallas_call(write_out, out_shape=(col, col, col, col, jax.ShapeDtypeSt...  0.79 us

profile of v3, /device:TPU:1, one launch (start us, length us, event | category | flops | bytes accessed | tf_op | source)
XLA Modules:
  0.0 35.1 jit_solution(2396628713185219223)
XLA Ops:
  0.6 33.7 %shard_map.155 = (f32[32,128]{1,0:T(8,128)S(1)}, f32[32,128]{1,0:T(8,128)S(1)}, f32[32,128]{1,0:T(8,128)S(1)}, f32[32,128]{1,0:T(8,128)S(1)}, f32[608,128]{1,0:T(8,128)S(1)}) custom-call(f32[32,128]{1,0:T(8,128)} %bitcast.20, f32[32,128]{1,0:T(8,128)} %bitcast.21, f32[32,128]{1,0:T(8,128)} %bitcast.22, f32[32,128]{1,0:T(8,128)} %bitcast.23, ...), custom_call_target="tpu_custom_call" | custom-call | tf_op jit(solution)/shard_map/pallas_call | solution.py:323
  34.3 0.8 %shard_map.156 = (f32[32,128]{1,0:T(8,128)}, f32[32,128]{1,0:T(8,128)}, f32[32,128]{1,0:T(8,128)}, f32[32,128]{1,0:T(8,128)}, f32[608,128]{1,0:T(8,128)}) custom-call(f32[32,128]{1,0:T(8,128)S(1)} %get-tuple-element.15.refs_0_, f32[32,128]{1,0:T(8,128)S(1)} %get-tuple-element.16.refs_1_, f32[32,128]{1,0:T(8,128)S(1)} %get-tuple-element.17.refs_2_, ...), custom_call_target="tpu_custom_call" | custom-call | tf_op jit(solution)/shard_map/pallas_call | solution.py:344

commit v4 on v3

--- a/solution.py
+++ b/solution.py
@@ -23,8 +23,9 @@
     u_hbm, v_hbm, t_hbm, s_hbm, q_hbm, c_hbm, dep_hbm, sol_hbm, a_hbm, ph_hbm, sat_hbm, pig_hbm,
     ou, ov, ot, osl, oc,
     a_s, ph_s, sat_s, pig_s, cin, oc_in, dep, sol, cs, hs, hn, zup_s, zdn_s, zup_r, zdn_r, xe_s, xw_s, xe_r, xw_r,
-    ps, pf, fs, fr, ush, uw, vsh, vsr, dpx, ops, mix, cw, ce, cu, cd,
-    loc, psend, precv, fsend, frecv, esend, erecv, nsend, nrecv, hsend, hrecv, dsend, drecv,
+    ps, pf, fs, fr, vsh, vsr, dpx, ops, mix, cw, ce, cu, cd,
+    pall, pws, pwr, psr, fs2, fr2, fqs, fqr, ep, ews, ewr, n2s, n2r, solx, wst,
+    loc, psend, precv, fsend, frecv, esend, erecv, nsend, nrecv, hsend, hrecv, dsend, drecv, xsend, xrecv,
 ):
     b = lax.axis_index("grp")
     ix = lax.axis_index("gx")
@@ -57,6 +58,9 @@
 
     lane8 = lax.broadcasted_iota(jnp.int32, (8, 128), 1)
     lane32 = lax.broadcasted_iota(jnp.int32, (32, 128), 1)
+    row8 = lax.broadcasted_iota(jnp.int32, (8, 128), 0)
+    row16 = lax.broadcasted_iota(jnp.int32, (16, 128), 0)
+    lane16 = lax.broadcasted_iota(jnp.int32, (16, 128), 1)
     row32 = lax.broadcasted_iota(jnp.int32, (32, 128), 0)
     sends = []
 
@@ -75,7 +79,7 @@
         else:
             pl.when(there)(copy.wait_recv)
 
-    for there, refs in ((has_w, (uw, xw_r)), (has_e, (xe_r,)), (has_s, (vsr, hs)), (has_n, (hn,))):
+    for there, refs in ((has_w, (ewr, xw_r, pwr, solx.at[0])), (has_e, (xe_r,)), (has_s, (vsr, hs, n2r, psr, solx.at[1])), (has_n, (hn,))):
 
         @pl.when(jnp.logical_not(there))
         def _():
@@ -94,15 +98,28 @@
             pig = pig + pig_s[i] * cs[t, i]
         for r in range(NG):
             ps[t, r] = pig[8 * r : 8 * r + 8]
-        pf[t, pl.ds(pl.multiple_of(b * 8, 8), 8), :] = ps[t, b]
         if t == 0:
+            pf[pl.ds(pl.multiple_of(b * 8, 8), 8), :] = ps[t, b]
             pl.semaphore_wait(barrier, NG - 1 + NG * sum(there.astype(jnp.int32) for there, _ in sides))
-        mine = pf.at[t, pl.ds(pl.multiple_of(b * 8, 8), 8), :]
-        for k, g in enumerate(peers):
-            send(ps.at[t, g], mine, psend.at[t, k], precv.at[t, b], {"grp": g})
+            for k, g in enumerate(peers):
+                send(ps.at[t, g], pf.at[pl.ds(pl.multiple_of(b * 8, 8), 8), :], psend.at[t, k], precv.at[t, b], {"grp": g})
+        else:
+            for k, g in enumerate(peers):
+                send(ps.at[t], pall.at[b], psend.at[t, k], precv.at[t, b], {"grp": g})
+            for g in range(NG):
+                send(ps.at[t, NG - 1], psr.at[b], xsend.at[0, g], xrecv.at[0, b], {"grp": g, **north}, has_n)
+            pack = jnp.zeros((8, 128), F32)
+            for r in range(NG):
+                pack = jnp.where(lane8 == r, roll(ps[t, r], r + 1, 1), pack)
+            pws[...] = pack
+            for g in range(NG):
+                send(pws, pwr.at[b], xsend.at[1, g], xrecv.at[1, b], {"grp": g, **east}, has_e)
+            pall[b] = ps[t]
         if t == 0:
             for k, (there, dev) in enumerate(sides):
                 send(dep_hbm, dpx.at[k ^ 1], dsend.at[k], drecv.at[k ^ 1], dev, there)
+            send(sol_hbm, solx.at[0], dsend.at[4], drecv.at[4], east, has_e)
+            send(sol_hbm, solx.at[1], dsend.at[5], drecv.at[5], north, has_n)
         send(cs.at[t, :, pl.ds(24, 8), :], hs.at[t], hsend.at[t, 0], hrecv.at[t, 0], north, has_n)
         send(cs.at[t, :, pl.ds(0, 8), :], hn.at[t], hsend.at[t, 1], hrecv.at[t, 1], south, has_s)
         pe = jnp.zeros((32, 128), F32)
@@ -137,22 +154,36 @@
 
         lax.fori_loop(0, NT, mixing, 0)
 
+    def bound(x):
+        return min(max(x, 0), 31)
+
+    def edges(hi, lo):
+        return jnp.where(row8 == 0, jnp.broadcast_to(hi, (8, 128)), jnp.broadcast_to(lo, (8, 128)))
+
+    def share_mixing():
+        for g in range(NG):
+            fqs[g, 0:8] = oc_in[4, 8 * g : 8 * g + 8]
+            fqs[g, 8:16] = edges(oc_in[4, bound(8 * g + 8) : bound(8 * g + 8) + 1], oc_in[4, bound(8 * g - 1) : bound(8 * g - 1) + 1])
+        for k, g in enumerate(peers):
+            send(fqs.at[g], fqr.at[b], xsend.at[2, k], xrecv.at[2, b], {"grp": g})
+        fqr[b] = fqs[b]
+
     def columns(t):
-        for k, g in enumerate(peers):
-            dst = pf.at[t, pl.ds(pl.multiple_of(g * 8, 8), 8), :]
-            arrived(dst, psend.at[t, k], precv.at[t, g])
-        att = 0.01 + 0.05 * pf[t]
+        if t == 0:
+            for k, g in enumerate(peers):
+                arrived(pf.at[pl.ds(pl.multiple_of(g * 8, 8), 8), :], psend.at[t, k], precv.at[t, g])
+            pig = pf[...]
+            u, v, temp, sal = (oc_in[n] for n in range(4))
+        else:
+            pig = jnp.concatenate([pall[g, b] for g in range(NG)], axis=0)
+            u, v, temp, sal = ou[...], ov[...], ot[...], osl[...]
+        att = 0.01 + 0.05 * pig
         cum = att
         for s in (1, 2, 4, 8, 16):
             cum = cum + jnp.where(row32 >= s, roll(cum, s, 0), 0.0)
         top = sol[pl.ds(b, 1), :] * jnp.exp(att - cum)
         heating = top * (1.0 - jnp.exp(-att))
-        par = top * jnp.exp(-0.5 * att)
         wet = (row32 < dep[pl.ds(b, 1), :]).astype(F32)
-        if t == 0:
-            u, v, temp, sal = (oc_in[n] for n in range(4))
-        else:
-            u, v, temp, sal = ou[...], ov[...], ot[...], osl[...]
         quiet = oc_in[4]
         temp = temp + 5.0 * heating * wet
         rho = 0.8 * sal - 0.2 * temp
@@ -165,24 +196,133 @@
             return x + flux - roll(flux, 1, 0)
 
         u, v, temp, sal = stir(u), stir(v), stir(temp), stir(sal)
-        above = roll(face, 1, 0)
+        if t == 0:
+            par = top * jnp.exp(-0.5 * att)
+            for n, x in enumerate((u, v, temp, face, roll(face, 1, 0), par)):
+                for g in range(NG):
+                    fs[g, n] = x[8 * g : 8 * g + 8]
+            for k, g in enumerate(peers):
+                send(fs.at[g], fr.at[b], fsend.at[0, k], frecv.at[0, b], {"grp": g})
+            vsh[...] = v
+            for g in range(NG):
+                send(vsh.at[pl.ds(8 * g, 8), :], vsr, nsend.at[0, g], nrecv.at[0], {"grp": g, **north}, jnp.logical_and(b == NG - 1, has_n))
+            pack = jnp.zeros((32, 128), F32)
+            for n, x in enumerate((u, temp, sal, quiet)):
+                pack = jnp.where(lane32 == n, roll(x, n + 1, 1), pack)
+            ep[...] = pack
+            for g in range(NG):
+                hi, lo = bound(8 * g + 8), bound(8 * g - 1)
+                ews[g, 0:8] = ep[8 * g : 8 * g + 8]
+                ews[g, 8:16] = edges(ep[hi : hi + 1], ep[lo : lo + 1])
+                send(ews.at[g], ewr.at[b], esend.at[g], erecv.at[b], {"grp": g, **east}, has_e)
+            fr[b] = fs[b]
         ou[...] = u
         ov[...] = v
         ot[...] = temp
         osl[...] = sal
-        warm = jnp.exp(0.0633 * (temp - 20.0))
-        for n, x in enumerate((u, v, warm, face, above, par)):
-            for g in range(NG):
-                fs[t, g, n] = x[8 * g : 8 * g + 8]
-        fr[t, b] = fs[t, b]
-        ush[t] = roll(u, 1, 1)
-        vsh[t] = v
+
+    def share_state():
+        for g in range(NG):
+            hi, lo = bound(8 * g + 8), bound(8 * g - 1)
+            fs2[g, 0] = osl[8 * g : 8 * g + 8]
+            for n, x in enumerate((ou, ov, ot, osl)):
+                fs2[g, 1, 2 * n : 2 * n + 1] = x[hi : hi + 1]
+                fs2[g, 1, 2 * n + 1 : 2 * n + 2] = x[lo : lo + 1]
         for k, g in enumerate(peers):
-            send(fs.at[t, g], fr.at[t, b], fsend.at[t, k], frecv.at[t, b], {"grp": g})
-
+            send(fs2.at[g], fr2.at[b], fsend.at[1, k], frecv.at[1, b], {"grp": g})
+        fr2[b] = fs2[b]
+        quiet = oc_in.at[4]
         for g in range(NG):
-            send(vsh.at[t, pl.ds(8 * g, 8), :], vsr.at[t], nsend.at[t, g], nrecv.at[t], {"grp": g, **north}, jnp.logical_and(b == NG - 1, has_n))
-            send(ush.at[t, pl.ds(8 * g, 8), :], uw.at[t, b], esend.at[t, g], erecv.at[t, b], {"grp": g, **east}, has_e)
+            hi, lo = bound(8 * g + 8), bound(8 * g - 1)
+            for n, x in enumerate((ot, osl, quiet)):
+                n2s[g, n] = x[8 * g : 8 * g + 8]
+            for n, x in enumerate((ov, ot, osl, quiet)):
+                n2s[g, 3, 2 * n : 2 * n + 1] = x[hi : hi + 1]
+                n2s[g, 3, 2 * n + 1 : 2 * n + 2] = x[lo : lo + 1]
+            send(n2s.at[g], n2r, nsend.at[1, g], nrecv.at[1], {"grp": g, **north}, jnp.logical_and(b == NG - 1, has_n))
+
+    def await_state():
+        for k, g in enumerate(peers):
+            arrived(fr2.at[g], fsend.at[1, k], frecv.at[1, g])
+            arrived(fqr.at[g], xsend.at[2, k], xrecv.at[2, g])
+        arrived(n2r, nsend.at[1, 0], nrecv.at[1], has_s)
+        arrived(solx.at[0], dsend.at[4], drecv.at[4], has_w)
+        arrived(solx.at[1], dsend.at[5], drecv.at[5], has_s)
+        for n in range(4):
+            x = jnp.zeros((16, 128), F32)
+            for r in range(NG):
+                x = jnp.where(lane16 == r, roll(ewr[r], r - n, 1), x)
+            wst[n] = x
+        for n, ref in ((4, dpx.at[0]), (5, solx.at[0])):
+            x = jnp.zeros((16, 128), F32)
+            for r in range(NG):
+                row = jnp.broadcast_to(ref[r : r + 1, :].astype(F32), (16, 128))
+                x = jnp.where(lane16 == r, roll(row, r + 1, 1), x)
+            wst[n] = x
+
+    def await_light():
+        for k, g in enumerate(peers):
+            arrived(pall.at[g], psend.at[1, k], precv.at[1, g])
+        for g in range(NG):
+            arrived(psr.at[g], xsend.at[0, g], xrecv.at[0, g], has_s)
+            arrived(pwr.at[g], xsend.at[1, g], xrecv.at[1, g], has_w)
+
+    def window(state, edge, n):
+        return jnp.concatenate([state, edges(edge[2 * n : 2 * n + 1, :], edge[2 * n + 1 : 2 * n + 2, :])], axis=0)
+
+    level16 = (jnp.where(row16 <= 8, row16, -1) + 8 * b).astype(F32)
+    has_above = jnp.logical_or(row16 <= 8, b > 0)
+
+    def band_ocean(pigment, surface, depth, temp, sal, quiet, movers):
+        att_of = lambda x: 0.01 + 0.05 * x
+        prefix = jnp.zeros((8, 128), F32)
+        for g in range(NG):
+            x = att_of(pigment(g))
+            for s in (4, 2, 1):
+                x = x + roll(x, s, 0)
+            prefix = prefix + jnp.where(g < b, x, 0.0)
+        own = att_of(pigment(b))
+        att_hi = att_of(pigment(jnp.minimum(b + 1, NG - 1))[0:1])
+        att_lo = att_of(pigment(jnp.maximum(b - 1, 0))[7:8])
+        cum = own
+        for s in (1, 2, 4):
+            cum = cum + jnp.where(row8 >= s, roll(cum, s, 0), 0.0)
+        att = jnp.concatenate([own, edges(att_hi, att_lo)], axis=0)
+        above = jnp.concatenate([prefix + (cum - own), prefix + edges(cum[7:8], -att_lo)], axis=0)
+        wet = jnp.where(level16 < depth, 1.0, 0.0)
+        top = surface * jnp.exp(-above)
+        temp = temp + 5.0 * (top * (1.0 - jnp.exp(-att))) * wet
+        rho = 0.8 * sal - 0.2 * temp
+        strat = roll(rho, 15, 0) - rho
+        face = (0.5 * (quiet + roll(quiet, 15, 0)) + 0.15 * jax.nn.sigmoid(-strat)) * roll(wet, 15, 0)
+        face = jnp.where(has_above, face, 0.0)
+
+        def stir(x):
+            flux = face * (roll(x, 15, 0) - x)
+            return (x + flux - roll(flux, 1, 0))[0:8]
+
+        par = top[0:8] * jnp.exp(-0.5 * own)
+        return [stir(x) for x in movers] + [stir(temp), face[0:8], roll(face, 1, 0)[0:8], par]
+
+    def forcing(t):
+        if t == 0:
+            got = [[fr[r, n] for n in range(NF)] for r in range(NG)]
+            west = [ewr[r, 0:8] for r in range(NG)]
+            south = vsr[...]
+        else:
+            wide = lambda x: jnp.broadcast_to(x.astype(F32), (16, 128))
+            got = []
+            for r in range(NG):
+                u, v, temp = (window(fr[r, n], fr2[r, 1], n) for n in range(3))
+                sal = window(fr2[r, 0], fr2[r, 1], 3)
+                got.append(band_ocean(lambda g: pall[g, r], wide(sol[r : r + 1, :]), wide(dep[r : r + 1, :]), temp, sal, fqr[r], (u, v)))
+            edge = n2r[3]
+            v = window(vsr[...], edge, 0)
+            temp, sal, quiet = (window(n2r[n], edge, n + 1) for n in range(3))
+            south = band_ocean(lambda g: psr[g], wide(solx[1, NG - 1 : NG, :]), wide(dpx[2, NG - 1 : NG, :]), temp, sal, quiet, (v,))[0]
+            uw = band_ocean(lambda g: pwr[g], wst[5], wst[4], wst[1], wst[2], wst[3], (wst[0],))[0]
+            west = [roll(uw, -r, 1) if r else uw for r in range(NG)]
+        return got, west, south
 
     def openings():
         for k in range(4):
@@ -232,15 +372,12 @@
                 cd[i, pl.ds(7, NG, stride=8), :] = zdn_r[t, i]
 
     def update(t):
-        for k, g in enumerate(peers):
-            arrived(fr.at[t, g], fsend.at[t, k], frecv.at[t, g])
-        for g in range(NG):
-            arrived(uw.at[t, g], esend.at[t, g], erecv.at[t, g], has_w)
-        arrived(vsr.at[t], nsend.at[t, 0], nrecv.at[t], has_s)
+        got, west, south = forcing(t)
         for r in range(NG):
-            u, v, warm, d, dm, par = (fr[t, r, n] for n in range(NF))
-            uwest = jnp.where(lane8 == 0, uw[t, r], roll(u, 1, 1))
-            vsouth = fr[t, r - 1, 1] if r > 0 else vsr[t]
+            u, v, temp, d, dm, par = got[r]
+            warm = jnp.exp(0.0633 * (temp - 20.0))
+            uwest = jnp.where(lane8 == 0, west[r], roll(u, 1, 1))
+            vsouth = got[r - 1][1] if r > 0 else south
             a_e = ops[0, r] * (jnp.maximum(u, 0.0) + 0.05)
             b_e = ops[0, r] * (0.05 - jnp.minimum(u, 0.0))
             a_w = ops[1, r] * (jnp.maximum(uwest, 0.0) + 0.05)
@@ -283,16 +420,25 @@
     publish(0)
     for copy in loads[1:8] + loads[9:]:
         copy.wait()
+    share_mixing()
     local_terms(0)
     openings()
     columns(0)
+    share_state()
     halos(0)
+    for k, g in enumerate(peers):
+        arrived(fr.at[g], fsend.at[0, k], frecv.at[0, g])
+    for g in range(NG):
+        arrived(ewr.at[g], esend.at[g], erecv.at[g], has_w)
+    arrived(vsr, nsend.at[0, 0], nrecv.at[0], has_s)
     update(0)
     publish(1)
     local_terms(1)
+    await_state()
+    halos(1)
+    await_light()
+    update(1)
     columns(1)
-    halos(1)
-    update(1)
 
     for there, copy in sends:
         if there is None:
@@ -331,13 +477,17 @@
             V((S, NT, 32, 128), F32), V((S, NT, 8, 128), F32), V((S, NT, 8, 128), F32),
             V((S, NT, 4, 128), F32), V((S, NT, 4, 128), F32), V((S, NT, 4, 128), F32), V((S, NT, 4, 128), F32),
             V((S, 32, 128), F32), V((S, 32, 128), F32), V((S, 32, 128), F32), V((S, 32, 128), F32),
-            V((S, NG, 8, 128), F32), V((S, 32, 128), F32),
-            V((S, NG, NF, 8, 128), F32), V((S, NG, NF, 8, 128), F32),
-            V((S, 32, 128), F32), V((S, NG, 8, 128), F32), V((S, 32, 128), F32), V((S, 8, 128), F32),
+            V((S, NG, 8, 128), F32), V((32, 128), F32),
+            V((NG, NF, 8, 128), F32), V((NG, NF, 8, 128), F32),
+            V((32, 128), F32), V((8, 128), F32),
             V((4, 4, 128), jnp.int32), V((5, NG, 8, 128), F32),
             V((NT, 32, 128), F32), V((NT, 32, 128), F32), V((NT, 32, 128), F32), V((NT, 32, 128), F32), V((NT, 32, 128), F32),
-            D((12,)), D((S, 3)), D((S, NG)), D((S, 3)), D((S, NG)), D((S, NG)), D((S, NG)), D((S, NG)), D((S,)),
-            D((S, 6)), D((S, 6)), D((4,)), D((4,)),
+            V((NG, NG, 8, 128), F32), V((8, 128), F32), V((NG, 8, 128), F32), V((NG, 8, 128), F32),
+            V((NG, 2, 8, 128), F32), V((NG, 2, 8, 128), F32), V((NG, 16, 128), F32), V((NG, 16, 128), F32),
+            V((32, 128), F32), V((NG, 16, 128), F32), V((NG, 16, 128), F32),
+            V((NG, 4, 8, 128), F32), V((4, 8, 128), F32), V((2, 4, 128), F32), V((6, 16, 128), F32),
+            D((12,)), D((S, 3)), D((S, NG)), D((S, 3)), D((S, NG)), D((NG,)), D((NG,)), D((S, NG)), D((S,)),
+            D((S, 6)), D((S, 6)), D((6,)), D((6,)), D((3, NG)), D((3, NG)),
         ],
         compiler_params=pltpu.CompilerParams(collective_id=0, has_side_effects=True, vmem_limit_bytes=16 << 20),
     )(*[pltpu.with_memory_space_constraint(x, pltpu.HBM) for x in (*fields, c.reshape(NT * 32, 128), dep, sol, rates, photo, satur, pig)])

time: 35.3 us -> 31.6 us (0.90)
  Pallas kernels: 34.5 us -> 30.8 us
    pallas_call x1, Pallas kernels: 33.7 us -> 30 us  [per_device(): pl.pallas_call(functools.partial(kernel, nx, ny), out_shape=(col, col, co...]
where the time goes in v4:
time: 31.6 us; the launch traced here: 31.5 us
  Pallas kernels  30.8 us (97%)
  between operations  0.64 us (2%)
    pallas_call x1, Pallas kernels, per_device(): pl.pallas_call(functools.partial(kernel, nx, ny), out_shape=(col, col, co...  30 us
    pallas_call x1, Pallas kernels, per_device(): pl.pallas_call(write_out, out_shape=(col, col, col, col, jax.ShapeDtypeSt...  0.79 us

profile of v4, /device:TPU:1, one launch (start us, length us, event | category | flops | bytes accessed | tf_op | source)
XLA Modules:
  0.0 31.5 jit_solution(9009833889852159123)
XLA Ops:
  0.6 30.0 %shard_map.155 = (f32[32,128]{1,0:T(8,128)S(1)}, f32[32,128]{1,0:T(8,128)S(1)}, f32[32,128]{1,0:T(8,128)S(1)}, f32[32,128]{1,0:T(8,128)S(1)}, f32[608,128]{1,0:T(8,128)S(1)}) custom-call(f32[32,128]{1,0:T(8,128)} %bitcast.20, f32[32,128]{1,0:T(8,128)} %bitcast.21, f32[32,128]{1,0:T(8,128)} %bitcast.22, f32[32,128]{1,0:T(8,128)} %bitcast.23, ...), custom_call_target="tpu_custom_call" | custom-call | tf_op jit(solution)/shard_map/pallas_call | solution.py:469
  30.7 0.8 %shard_map.156 = (f32[32,128]{1,0:T(8,128)}, f32[32,128]{1,0:T(8,128)}, f32[32,128]{1,0:T(8,128)}, f32[32,128]{1,0:T(8,128)}, f32[608,128]{1,0:T(8,128)}) custom-call(f32[32,128]{1,0:T(8,128)S(1)} %get-tuple-element.15.refs_0_, f32[32,128]{1,0:T(8,128)S(1)} %get-tuple-element.16.refs_1_, f32[32,128]{1,0:T(8,128)S(1)} %get-tuple-element.17.refs_2_, ...), custom_call_target="tpu_custom_call" | custom-call | tf_op jit(solution)/shard_map/pallas_call | solution.py:494

commit v5 on v4

v5 whole, which is shorter than its diff:
```python
import functools

import jax
import jax.numpy as jnp
from jax import lax
from jax.experimental import pallas as pl
from jax.experimental.pallas import tpu as pltpu
from jax.sharding import PartitionSpec as P

STEPS = 2
NG = 4
NT = 19
F32 = jnp.float32
NF = 3
SEND = ("pig", "dep0", "dep1", "dep2", "dep3", "solw", "sols", "h0", "h1", "h2", "h3", "h4", "h5", "fixed", "force", "edge", "state", "v", "row", "u", "col", "sums", "ssum", "wsum", "span", "wpan", "cols")
RECV = SEND[:7] + tuple(f"h{n}{t}" for n in range(6) for t in range(2)) + SEND[13:]


def roll(x, shift, axis):
    return pltpu.roll(x, shift % x.shape[axis], axis)


def kernel(
    nx, ny,
    u_hbm, v_hbm, t_hbm, s_hbm, q_hbm, c_hbm, dep_hbm, sol_hbm, a_hbm, ph_hbm, sat_hbm, pig_hbm,
    ou, ov, ot, osl, oc,
    a_s, ph_s, sat_s, pig_s, cin, oc_in, dep, sol, cs, hs, hn, zup_s, zdn_s, zup_r, zdn_r, xe_s, xw_s, xe_r, xw_r,
    ps, pf, fs, fr, vsh, vsr, dpx, ops, mix, cw, ce, cu, cd,
    uv, dls, dlr, pcs, pcr, scs, scr, wcs, wcr, pws, pwr, psr, fs2, fr2, fqs, fqr, ep, ews, ewr, ewx, n2s, n2r, solx, wst,
    loc, ssems, rsems,
):
    b = lax.axis_index("grp")
    ix = lax.axis_index("gx")
    iy = lax.axis_index("gy")
    has_e, has_w, has_n, has_s = ix < nx - 1, ix > 0, iy < ny - 1, iy > 0
    east, west, north, south = {"gx": ix + 1}, {"gx": ix - 1}, {"gy": iy + 1}, {"gy": iy - 1}
    sides = ((has_w, west), (has_e, east), (has_s, south), (has_n, north))
    peers = [lax.rem(b + k, NG) for k in (2, 3, 1)]

    loads = [pltpu.make_async_copy(c_hbm, cin, loc.at[0])]
    for n, (ref, dst) in enumerate(((pig_hbm, pig_s), (dep_hbm, dep), (sol_hbm, sol), (a_hbm, a_s), (ph_hbm, ph_s), (sat_hbm, sat_s))):
        loads.append(pltpu.make_async_copy(ref, dst, loc.at[1 + n]))
    for n, ref in enumerate((u_hbm, v_hbm, t_hbm, s_hbm, q_hbm)):
        loads.append(pltpu.make_async_copy(ref, oc_in.at[n], loc.at[7]))
    for copy in loads:
        copy.start()

    barrier = pltpu.get_barrier_semaphore()
    for g in peers:
        pl.semaphore_signal(barrier, inc=1, device_id={"grp": g})
    for there, dev in sides[::-1]:

        @pl.when(there)
        def _():
            for g in range(NG):
                pl.semaphore_signal(barrier, inc=1, device_id={"grp": g, **dev})

    lane8 = lax.broadcasted_iota(jnp.int32, (8, 128), 1)
    lane32 = lax.broadcasted_iota(jnp.int32, (32, 128), 1)
    row8 = lax.broadcasted_iota(jnp.int32, (8, 128), 0)
    row16 = lax.broadcasted_iota(jnp.int32, (16, 128), 0)
    lane16 = lax.broadcasted_iota(jnp.int32, (16, 128), 1)
    row32 = lax.broadcasted_iota(jnp.int32, (32, 128), 0)
    pending = []

    def remote(src, dst, name, dev):
        tag, at = (name[:2], name) if name[0] == "h" else (name, name)
        return pltpu.make_async_remote_copy(src, dst, ssems.at[SEND.index(tag)], rsems.at[RECV.index(at)], device_id=dev, device_id_type=pl.DeviceIdType.MESH)

    def guarded(there, act):
        if there is None:
            act()
        else:
            pl.when(there)(act)

    def send(src, dst, name, dev, there=None, whole=None):
        if whole is not False:
            pending.append((there, src if whole is None else whole, name))
        guarded(there, remote(src, dst, name, dev).start)

    def sent(names=None):
        for there, ref, name in pending:
            if names is None or name in names:
                guarded(there, remote(ref, ref, name, {"grp": peers[0]}).wait_send)
        pending[:] = [x for x in pending if names is not None and x[2] not in names]

    def arrived(ref, name, there=None):
        guarded(there, remote(ref, ref, name, {"grp": peers[0]}).wait_recv)

    def first(k, ref):
        return ref if k == 0 else False

    for there, refs in ((has_w, (ewr, ewx, xw_r, pwr, wcr, solx.at[0])), (has_e, (xe_r,)), (has_s, (vsr, hs, n2r, psr, scr, solx.at[1])), (has_n, (hn,))):

        @pl.when(jnp.logical_not(there))
        def _():
            for ref in refs:
                ref[...] = jnp.zeros_like(ref)

    for k, (there, _) in enumerate(sides):

        @pl.when(jnp.logical_not(there))
        def _():
            dpx[k] = jnp.zeros((4, 128), jnp.int32)

    def publish(t):
        pig = jnp.zeros((32, 128), F32)
        for i in range(NT):
            pig = pig + pig_s[i] * cs[t, i]
        for r in range(NG):
            ps[t, r] = pig[8 * r : 8 * r + 8]
        pf[t, pl.ds(pl.multiple_of(b * 8, 8), 8), :] = ps[t, b]
        mine = pf.at[t, pl.ds(pl.multiple_of(b * 8, 8), 8), :]
        if t == 0:
            pl.semaphore_wait(barrier, NG - 1 + NG * sum(there.astype(jnp.int32) for there, _ in sides))
            for k, g in enumerate(peers):
                send(ps.at[t, g], mine, "pig", {"grp": g}, whole=first(k, ps.at[t, 0:3]))
        else:
            def total(x):
                for n in (4, 2, 1):
                    x = x + roll(x, n, 0)
                return x[0:1]

            for r in range(NG):
                x = 0.01 + 0.05 * ps[t, r]
                whole = total(x)
                for n, edge in enumerate((x[7:8], x[0:1])):
                    pcs[n, r : r + 1] = whole
                    pcs[n, NG + r : NG + r + 1] = edge
            pack = jnp.zeros((8, 128), F32)
            for r in range(NG):
                pack = jnp.where(lane8 == r, roll(ps[t, r], r + 1, 1), pack)
            pws[...] = pack
            for ref, x in ((scs, ps[t, NG - 1]), (wcs, pack)):
                x = 0.01 + 0.05 * x
                whole = total(x)
                for n, edge in enumerate((x[7:8], x[0:1])):
                    ref[n, 0:1] = whole
                    ref[n, 1:2] = edge
            for k, g in enumerate(peers):
                send(pcs.at[(g < b).astype(jnp.int32)], pcr.at[b], "sums", {"grp": g}, whole=first(k, pcr.at[0:3]))
            for k, g in enumerate(peers):
                side = (g < b).astype(jnp.int32)
                send(scs.at[side], scr.at[b], "ssum", {"grp": g, **north}, has_n, first(k, scr.at[0:3]))
                send(wcs.at[side], wcr.at[b], "wsum", {"grp": g, **east}, has_e, first(k, wcr.at[0:3]))
            send(ps.at[t, NG - 1], psr, "span", north, has_n)
            send(pws, pwr, "wpan", east, has_e)
            pcr[b] = pcs[0]
            scr[b] = scs[0]
            wcr[b] = wcs[0]
        if t == 0:
            for k, (there, dev) in enumerate(sides):
                send(dep_hbm, dpx.at[k ^ 1], f"dep{k ^ 1}", dev, there)
            send(sol_hbm, solx.at[0], "solw", east, has_e)
            send(sol_hbm, solx.at[1], "sols", north, has_n)
        if t == 1:
            sent([f"h{n}0" for n in range(6)])
        send(cs.at[t, :, pl.ds(24, 8), :], hs.at[t], f"h0{t}", north, has_n)
        send(cs.at[t, :, pl.ds(0, 8), :], hn.at[t], f"h1{t}", south, has_s)
        pe = jnp.zeros((32, 128), F32)
        pw = jnp.zeros((32, 128), F32)
        for i in range(NT):
            x = cs[t, i]
            pe = jnp.where(lane32 == i, roll(x, i + 1, 1), pe)
            pw = jnp.where(lane32 == i, roll(x, i, 1) if i else x, pw)
        xe_s[t] = pe
        xw_s[t] = pw
        send(xe_s.at[t], xw_r.at[t], f"h2{t}", east, has_e)
        send(xw_s.at[t], xe_r.at[t], f"h3{t}", west, has_w)
        for i in range(NT):
            zup_s[t, i] = cs[t, i, pl.ds(7, NG, stride=8), :]
            zdn_s[t, i] = cs[t, i, pl.ds(0, NG, stride=8), :]

        send(zup_s.at[t], zup_r.at[t], f"h4{t}", {"grp": b + 1}, b < NG - 1)
        send(zdn_s.at[t], zdn_r.at[t], f"h5{t}", {"grp": b - 1}, b > 0)
        if t == 1:
            for k, g in enumerate(peers):
                send(ps.at[t, g], mine, "cols", {"grp": g}, whole=first(k, ps.at[t, 0:3]))

    def local_terms(t):
        def mixing(i, _):
            acc = a_s[i, 0] * cs[t, 0]
            for j in range(1, NT):
                acc = acc + a_s[i, j] * cs[t, j]
            mix[i] = acc
            x = cs[t, i]
            cw[i] = roll(x, 1, 1)
            ce[i] = roll(x, 127, 1)
            cu[i] = roll(x, 1, 0)
            cd[i] = roll(x, 31, 0)
            return 0

        lax.fori_loop(0, NT, mixing, 0)

    def bound(x):
        return min(max(x, 0), 31)

    def edges(hi, lo):
        return jnp.where(row8 == 0, jnp.broadcast_to(hi, (8, 128)), jnp.broadcast_to(lo, (8, 128)))

    def share_fixed():
        for g in range(NG):
            hi, lo = bound(8 * g + 8), bound(8 * g - 1)
            for n, x in enumerate((0, 1, 4)):
                fqs[g, n] = oc_in[x, 8 * g : 8 * g + 8]
            for n, x in enumerate((0, 1, 4, 4)):
                fqs[g, 3, 2 * n : 2 * n + 1] = oc_in[x, hi : hi + 1]
                fqs[g, 3, 2 * n + 1 : 2 * n + 2] = oc_in[x, lo : lo + 1]
        for k, g in enumerate(peers):
            send(fqs.at[g], fqr.at[b], "fixed", {"grp": g}, whole=first(k, fqs.at[0:3]))
        fqr[b] = fqs[b]

    def columns(t):
        if t == 0:
            arrived(pf.at[t, 0:24], "pig")
            u, v, temp, sal = (oc_in[n] for n in range(4))
        else:
            u, v, temp, sal = ou[...], ov[...], ot[...], osl[...]
        att = 0.01 + 0.05 * pf[t]
        cum = att
        for s in (1, 2, 4, 8, 16):
            cum = cum + jnp.where(row32 >= s, roll(cum, s, 0), 0.0)
        top = sol[pl.ds(b, 1), :] * jnp.exp(att - cum)
        heating = top * (1.0 - jnp.exp(-att))
        wet = (row32 < dep[pl.ds(b, 1), :]).astype(F32)
        quiet = oc_in[4]
        temp = temp + 5.0 * heating * wet
        rho = 0.8 * sal - 0.2 * temp
        strat = roll(rho, 31, 0) - rho
        face = (0.5 * (quiet + roll(quiet, 31, 0)) + 0.15 * jax.nn.sigmoid(-strat)) * roll(wet, 31, 0)
        face = jnp.where(row32 < 31, face, 0.0)

        def stir(x):
            flux = face * (roll(x, 31, 0) - x)
            return x + flux - roll(flux, 1, 0)

        u, v, temp, sal = stir(u), stir(v), stir(temp), stir(sal)
        if t == 0:
            par = top * jnp.exp(-0.5 * att)
            for n, x in enumerate((temp, face, par)):
                for g in range(NG):
                    fs[g, n] = x[8 * g : 8 * g + 8]
            dls[0] = jnp.zeros((1, 128), F32)
            for g in range(1, NG):
                dls[g] = face[8 * g - 1 : 8 * g]
            for k, g in enumerate(peers):
                send(fs.at[g], fr.at[b], "force", {"grp": g}, whole=first(k, fs.at[0:3]))
                send(dls.at[g], dlr.at[b], "edge", {"grp": g}, whole=first(k, dls.at[0:3]))
            vsh[...] = v
            for g in range(NG):
                send(vsh.at[pl.ds(8 * g, 8), :], vsr, "v", {"grp": g, **north}, jnp.logical_and(b == NG - 1, has_n), first(g, vsh))
            pack = jnp.zeros((32, 128), F32)
            for n, x in enumerate((u, temp, sal, quiet)):
                pack = jnp.where(lane32 == n, roll(x, n + 1, 1), pack)
            ep[...] = pack
            for g in range(NG):
                send(ep.at[8 * g : 8 * g + 8], ewr.at[b], "u", {"grp": g, **east}, has_e, first(g, ep))
            fr[b] = fs[b]
            dlr[b] = dls[b]
        ou[...] = u
        ov[...] = v
        ot[...] = temp
        osl[...] = sal

    def share_state():
        for g in range(NG):
            hi, lo = bound(8 * g + 8), bound(8 * g - 1)
            fs2[g, 0] = osl[8 * g : 8 * g + 8]
            for n, x in enumerate((ou, ov, ot, osl)):
                fs2[g, 1, 2 * n : 2 * n + 1] = x[hi : hi + 1]
                fs2[g, 1, 2 * n + 1 : 2 * n + 2] = x[lo : lo + 1]
        for k, g in enumerate(peers):
            send(fs2.at[g], fr2.at[b], "state", {"grp": g}, whole=first(k, fs2.at[0:3]))
        fr2[b] = fs2[b]
        for g in range(NG):
            hi, lo = bound(8 * g + 8), bound(8 * g - 1)
            ews[g] = edges(ep[hi : hi + 1], ep[lo : lo + 1])
            send(ews.at[g], ewx.at[b], "col", {"grp": g, **east}, has_e, first(g, ews))
        quiet = oc_in.at[4]
        for g in range(NG):
            hi, lo = bound(8 * g + 8), bound(8 * g - 1)
            for n, x in enumerate((ot, osl, quiet)):
                n2s[g, n] = x[8 * g : 8 * g + 8]
            for n, x in enumerate((ov, ot, osl, quiet)):
                n2s[g, 3, 2 * n : 2 * n + 1] = x[hi : hi + 1]
                n2s[g, 3, 2 * n + 1 : 2 * n + 2] = x[lo : lo + 1]
            send(n2s.at[g], n2r, "row", {"grp": g, **north}, jnp.logical_and(b == NG - 1, has_n), first(g, n2s))

    def await_state():
        arrived(fr2.at[0:3], "state")
        arrived(ewx, "col", has_w)
        arrived(n2r, "row", has_s)
        arrived(solx.at[0], "solw", has_w)
        arrived(solx.at[1], "sols", has_s)
        for n in range(4):
            x = jnp.zeros((16, 128), F32)
            for r in range(NG):
                x = jnp.where(lane16 == r, roll(jnp.concatenate([ewr[r], ewx[r]], axis=0), r - n, 1), x)
            wst[n] = x
        for n, ref in ((4, dpx.at[0]), (5, solx.at[0])):
            x = jnp.zeros((16, 128), F32)
            for r in range(NG):
                row = jnp.broadcast_to(ref[r : r + 1, :].astype(F32), (16, 128))
                x = jnp.where(lane16 == r, roll(row, r + 1, 1), x)
            wst[n] = x

    def await_light():
        arrived(pcr.at[0:3], "sums")
        arrived(scr.at[0:3], "ssum", has_s)
        arrived(wcr.at[0:3], "wsum", has_w)
        arrived(pf.at[1, 0:24], "cols")
        arrived(psr, "span", has_s)
        arrived(pwr, "wpan", has_w)

    def window(state, edge, n):
        return jnp.concatenate([state, edges(edge[2 * n : 2 * n + 1, :], edge[2 * n + 1 : 2 * n + 2, :])], axis=0)

    level16 = (jnp.where(row16 <= 8, row16, -1) + 8 * b).astype(F32)
    has_above = jnp.logical_or(row16 <= 8, b > 0)

    below, over = jnp.minimum(b + 1, NG - 1), jnp.maximum(b - 1, 0)

    def band_ocean(pigment, total, edge, surface, depth, temp, sal, quiet, movers):
        prefix = jnp.zeros((1, 128), F32)
        for g in range(NG):
            prefix = prefix + jnp.where(g < b, total(g), 0.0)
        prefix = jnp.broadcast_to(prefix, (8, 128))
        own = 0.01 + 0.05 * pigment
        att_hi, att_lo = edge(below), edge(over)
        cum = own
        for s in (1, 2, 4):
            cum = cum + jnp.where(row8 >= s, roll(cum, s, 0), 0.0)
        att = jnp.concatenate([own, edges(att_hi, att_lo)], axis=0)
        above = jnp.concatenate([prefix + (cum - own), prefix + edges(cum[7:8], -att_lo)], axis=0)
        wet = jnp.where(level16 < depth, 1.0, 0.0)
        top = surface * jnp.exp(-above)
        temp = temp + 5.0 * (top * (1.0 - jnp.exp(-att))) * wet
        rho = 0.8 * sal - 0.2 * temp
        strat = roll(rho, 15, 0) - rho
        face = (0.5 * (quiet + roll(quiet, 15, 0)) + 0.15 * jax.nn.sigmoid(-strat)) * roll(wet, 15, 0)
        face = jnp.where(has_above, face, 0.0)

        def stir(x):
            flux = face * (roll(x, 15, 0) - x)
            return (x + flux - roll(flux, 1, 0))[0:8]

        par = top[0:8] * jnp.exp(-0.5 * own)
        return [stir(x) for x in movers] + [stir(temp), face[0:8], roll(face, 1, 0)[0:8], par]

    def forcing(t):
        got = []
        if t == 0:
            for r in range(NG):
                temp, d, par = (fr[r, n] for n in range(NF))
                dm = jnp.where(row8 == 0, jnp.broadcast_to(dlr[r], (8, 128)), roll(d, 1, 0))
                moved = []
                for n in range(2):
                    x = fqr[r, n]
                    hi = jnp.broadcast_to(fqr[r, 3, 2 * n : 2 * n + 1], (8, 128))
                    lo = jnp.broadcast_to(fqr[r, 3, 2 * n + 1 : 2 * n + 2], (8, 128))
                    x = x + d * (jnp.where(row8 == 7, hi, roll(x, 7, 0)) - x) - dm * (x - jnp.where(row8 == 0, lo, roll(x, 1, 0)))
                    uv[r, n] = x
                    moved.append(x)
                got.append(moved + [temp, d, dm, par])
            west = [ewr[r] for r in range(NG)]
            south = vsr[...]
        else:
            wide = lambda x: jnp.broadcast_to(x.astype(F32), (16, 128))
            for r in range(NG):
                u, v = (window(uv[r, n], fr2[r, 1], n) for n in range(2))
                temp = window(fr[r, 0], fr2[r, 1], 2)
                sal = window(fr2[r, 0], fr2[r, 1], 3)
                quiet = window(fqr[r, 2], fqr[r, 3], 2)
                got.append(band_ocean(ps[1, r], lambda g: pcr[g, r : r + 1], lambda g: pcr[g, NG + r : NG + r + 1], wide(sol[r : r + 1, :]), wide(dep[r : r + 1, :]), temp, sal, quiet, (u, v)))
            edge = n2r[3]
            v = window(vsr[...], edge, 0)
            temp, sal, quiet = (window(n2r[n], edge, n + 1) for n in range(3))
            south = band_ocean(psr[...], lambda g: scr[g, 0:1], lambda g: scr[g, 1:2], wide(solx[1, NG - 1 : NG, :]), wide(dpx[2, NG - 1 : NG, :]), temp, sal, quiet, (v,))[0]
            uw = band_ocean(pwr[...], lambda g: wcr[g, 0:1], lambda g: wcr[g, 1:2], wst[5], wst[4], wst[1], wst[2], wst[3], (wst[0],))[0]
            west = [roll(uw, -r, 1) if r else uw for r in range(NG)]
        return got, west, south

    def openings():
        for k in range(4):
            arrived(dpx.at[k], f"dep{k}", sides[k][0])
        level = (lax.broadcasted_iota(jnp.int32, (8, 128), 0) + 8 * b).astype(F32)

        def wet_of(rows):
            return jnp.where(level < jnp.broadcast_to(rows, (8, 128)), 1.0, 0.0)

        def row(ref, r):
            return jnp.broadcast_to(ref[r : r + 1, :].astype(F32), (8, 128))

        own = [row(dep, r) for r in range(NG)]
        wets = [wet_of(x) for x in own]
        wet_n = wet_of(row(dpx.at[3], 0))
        wet_s = wet_of(row(dpx.at[2], NG - 1))
        for r in range(NG):
            wet_e = jnp.where(lane8 == 127, roll(wet_of(row(dpx.at[1], r)), 127, 1), roll(wets[r], 127, 1))
            wet_w = jnp.where(lane8 == 0, roll(wet_of(row(dpx.at[0], r)), 1, 1), roll(wets[r], 1, 1))
            ops[0, r] = wets[r] * wet_e
            ops[1, r] = wets[r] * wet_w
            ops[2, r] = wets[r] * (wets[r + 1] if r < NG - 1 else wet_n)
            ops[3, r] = wets[r] * (wets[r - 1] if r > 0 else wet_s)
            ops[4, r] = 0.5 * wets[r]

    def halos(t):
        arrived(hs.at[t], f"h0{t}", has_s)
        arrived(hn.at[t], f"h1{t}", has_n)
        arrived(xw_r.at[t], f"h2{t}", has_w)
        arrived(xe_r.at[t], f"h3{t}", has_e)
        pw = xw_r[t]
        pe = xe_r[t]
        for i in range(NT):
            cw[i] = jnp.where(lane32 == 0, roll(pw, 128 - i, 1) if i else pw, cw[i])
            ce[i] = jnp.where(lane32 == 127, roll(pe, 127 - i, 1), ce[i])

        @pl.when(b > 0)
        def _():
            arrived(zup_r.at[t], f"h4{t}")
            for i in range(NT):
                cu[i, pl.ds(0, NG, stride=8), :] = zup_r[t, i]

        @pl.when(b < NG - 1)
        def _():
            arrived(zdn_r.at[t], f"h5{t}")
            for i in range(NT):
                cd[i, pl.ds(7, NG, stride=8), :] = zdn_r[t, i]

    def update(t):
        got, west, south = forcing(t)
        for r in range(NG):
            u, v, temp, d, dm, par = got[r]
            warm = jnp.exp(0.0633 * (temp - 20.0))
            uwest = jnp.where(lane8 == 0, west[r], roll(u, 1, 1))
            vsouth = got[r - 1][1] if r > 0 else south
            a_e = ops[0, r] * (jnp.maximum(u, 0.0) + 0.05)
            b_e = ops[0, r] * (0.05 - jnp.minimum(u, 0.0))
            a_w = ops[1, r] * (jnp.maximum(uwest, 0.0) + 0.05)
            b_w = ops[1, r] * (0.05 - jnp.minimum(uwest, 0.0))
            a_n = ops[2, r] * (jnp.maximum(v, 0.0) + 0.05)
            b_n = ops[2, r] * (0.05 - jnp.minimum(v, 0.0))
            a_s_ = ops[3, r] * (jnp.maximum(vsouth, 0.0) + 0.05)
            b_s = ops[3, r] * (0.05 - jnp.minimum(vsouth, 0.0))
            k0 = 1.0 - a_e - b_w - a_n - b_s - d - dm
            half = ops[4, r]
            warm = half * warm
            parw = half * par
            rows = pl.ds(8 * r, 8)

            def one(i, _):
                x = cs[t, i, rows, :]
                up = cs[t, i, pl.ds(8 * r + 8, 8), :] if r < NG - 1 else hn[t, i]
                dn = cs[t, i, pl.ds(8 * r - 8, 8), :] if r > 0 else hs[t, i]
                grow = k0 + ph_s[i] * parw / (par + sat_s[i])
                new = (
                    grow * x
                    + (b_e * ce[i, rows, :] + a_w * cw[i, rows, :])
                    + (b_n * up + a_s_ * dn)
                    + (d * cd[i, rows, :] + dm * cu[i, rows, :])
                    + warm * mix[i, rows, :]
                )
                if t == STEPS - 1:
                    oc[pl.ds(i * 32 + r, 8, stride=4), :] = new
                else:
                    cs[t + 1, i, rows, :] = new
                return 0

            lax.fori_loop(0, NT, one, 0, unroll=True)

    loads[0].wait()
    for i in range(NT):
        for r in range(NG):
            cs[0, i, pl.ds(8 * r, 8), :] = cin[pl.ds(i * 32 + r, 8, stride=4), :]
    loads[1].wait()
    publish(0)
    for copy in loads[2:7] + [pltpu.make_async_copy(oc_in, oc_in, loc.at[7])]:
        copy.wait()
    share_fixed()
    local_terms(0)
    columns(0)
    share_state()
    openings()
    halos(0)
    arrived(fqr.at[0:3], "fixed")
    arrived(fr.at[0:3], "force")
    arrived(dlr.at[0:3], "edge")
    arrived(ewr, "u", has_w)
    arrived(vsr, "v", has_s)
    update(0)
    publish(1)
    local_terms(1)
    await_state()
    halos(1)
    await_light()
    update(1)
    columns(1)

    sent()


def write_out(*refs):
    n = (len(refs) - 1) // 2
    copies = [pltpu.make_async_copy(refs[k], refs[n + k], refs[-1].at[k]) for k in range(n)]
    for copy in copies:
        copy.start()
    for copy in copies:
        copy.wait()


def per_device(nx, ny, *args):
    u, v, temp, sal, quiet, c, dep, sol, rates, photo, satur, pig = args
    shape = u.shape
    fields = [x.reshape(32, 128) for x in (u, v, temp, sal, quiet)]
    hbm = pl.BlockSpec(memory_space=pltpu.HBM)
    vmem = pl.BlockSpec(memory_space=pltpu.VMEM)
    col = jax.ShapeDtypeStruct((32, 128), F32)
    V = pltpu.VMEM
    D = pltpu.SemaphoreType.DMA
    S = STEPS
    out = pl.pallas_call(
        functools.partial(kernel, nx, ny),
        out_shape=(col, col, col, col, jax.ShapeDtypeStruct((NT * 32, 128), F32)),
        in_specs=[hbm] * 12,
        out_specs=(vmem,) * 5,
        scratch_shapes=[
            pltpu.SMEM((NT, NT), F32), pltpu.SMEM((NT,), F32), pltpu.SMEM((NT,), F32), pltpu.SMEM((NT,), F32),
            V((NT * 32, 128), F32), V((5, 32, 128), F32), V((4, 128), jnp.int32), V((4, 128), F32),
            V((S, NT, 32, 128), F32), V((S, NT, 8, 128), F32), V((S, NT, 8, 128), F32),
            V((S, NT, 4, 128), F32), V((S, NT, 4, 128), F32), V((S, NT, 4, 128), F32), V((S, NT, 4, 128), F32),
            V((S, 32, 128), F32), V((S, 32, 128), F32), V((S, 32, 128), F32), V((S, 32, 128), F32),
            V((S, NG, 8, 128), F32), V((S, 32, 128), F32),
            V((NG, NF, 8, 128), F32), V((NG, NF, 8, 128), F32),
            V((32, 128), F32), V((8, 128), F32),
            V((4, 4, 128), jnp.int32), V((5, NG, 8, 128), F32),
            V((NT, 32, 128), F32), V((NT, 32, 128), F32), V((NT, 32, 128), F32), V((NT, 32, 128), F32), V((NT, 32, 128), F32),
            V((NG, 2, 8, 128), F32), V((NG, 1, 128), F32), V((NG, 1, 128), F32), V((2, 8, 128), F32), V((NG, 8, 128), F32),
            V((2, 2, 128), F32), V((NG, 2, 128), F32), V((2, 2, 128), F32), V((NG, 2, 128), F32),
            V((8, 128), F32), V((8, 128), F32), V((8, 128), F32),
            V((NG, 2, 8, 128), F32), V((NG, 2, 8, 128), F32), V((NG, 4, 8, 128), F32), V((NG, 4, 8, 128), F32),
            V((32, 128), F32), V((NG, 8, 128), F32), V((NG, 8, 128), F32), V((NG, 8, 128), F32),
            V((NG, 4, 8, 128), F32), V((4, 8, 128), F32), V((2, 4, 128), F32), V((6, 16, 128), F32),
            D((8,)), D((len(SEND),)), D((len(RECV),)),
        ],
        compiler_params=pltpu.CompilerParams(collective_id=0, has_side_effects=True, vmem_limit_bytes=16 << 20),
    )(*[pltpu.with_memory_space_constraint(x, pltpu.HBM) for x in (*fields, c.reshape(NT * 32, 128), dep, sol, rates, photo, satur, pig)])
    out = pl.pallas_call(
        write_out,
        out_shape=(col, col, col, col, jax.ShapeDtypeStruct((NT * 32, 128), F32)),
        in_specs=[vmem] * 5,
        out_specs=(hbm,) * 5,
        scratch_shapes=[D((5,))],
        compiler_params=pltpu.CompilerParams(vmem_limit_bytes=4 << 20),
    )(*out)
    return tuple(x.reshape(shape) for x in out[:4]) + (out[4].reshape(c.shape),)


def solution(mesh):
    field = P(None, "gy", "grp", "gx")
    tracer = P(None, "grp", "gy", "gx")
    flat = P("gy", "gx")
    return jax.shard_map(
        functools.partial(per_device, mesh.shape["gx"], mesh.shape["gy"]),
        mesh=mesh,
        in_specs=(field,) * 5 + (tracer, flat, flat, P(), P(), P(), P()),
        out_specs=(field,) * 4 + (tracer,),
        check_vma=False,
    )
```

time: 31.6 us -> 30.9 us (0.978)
  Pallas kernels: 30.8 us -> 30.1 us
    pallas_call x1, Pallas kernels: 30 us -> 29.3 us  [per_device(): pl.pallas_call(functools.partial(kernel, nx, ny), out_shape=(col, col, co...]
where the time goes in v5:
time: 30.9 us; the launch traced here: 30.7 us
  Pallas kernels  30.1 us (97%)
  between operations  0.64 us (2%)
    pallas_call x1, Pallas kernels, per_device(): pl.pallas_call(functools.partial(kernel, nx, ny), out_shape=(col, col, co...  29.3 us
    pallas_call x1, Pallas kernels, per_device(): pl.pallas_call(write_out, out_shape=(col, col, col, col, jax.ShapeDtypeSt...  0.79 us

profile of v5, /device:TPU:1, one launch (start us, length us, event | category | flops | bytes accessed | tf_op | source)
XLA Modules:
  0.0 30.7 jit_solution(7871645211556115470)
XLA Ops:
  0.6 29.3 %shard_map.155 = (f32[32,128]{1,0:T(8,128)S(1)}, f32[32,128]{1,0:T(8,128)S(1)}, f32[32,128]{1,0:T(8,128)S(1)}, f32[32,128]{1,0:T(8,128)S(1)}, f32[608,128]{1,0:T(8,128)S(1)}) custom-call(f32[32,128]{1,0:T(8,128)} %bitcast.20, f32[32,128]{1,0:T(8,128)} %bitcast.21, f32[32,128]{1,0:T(8,128)} %bitcast.22, f32[32,128]{1,0:T(8,128)} %bitcast.23, ...), custom_call_target="tpu_custom_call" | custom-call | tf_op jit(solution)/shard_map/pallas_call | solution.py:521
  29.9 0.8 %shard_map.156 = (f32[32,128]{1,0:T(8,128)}, f32[32,128]{1,0:T(8,128)}, f32[32,128]{1,0:T(8,128)}, f32[32,128]{1,0:T(8,128)}, f32[608,128]{1,0:T(8,128)}) custom-call(f32[32,128]{1,0:T(8,128)S(1)} %get-tuple-element.15.refs_0_, f32[32,128]{1,0:T(8,128)S(1)} %get-tuple-element.16.refs_1_, f32[32,128]{1,0:T(8,128)S(1)} %get-tuple-element.17.refs_2_, ...), custom_call_target="tpu_custom_call" | custom-call | tf_op jit(solution)/shard_map/pallas_call | solution.py:547

commit v6 on v5

--- a/solution.py
+++ b/solution.py
@@ -26,7 +26,7 @@
     ou, ov, ot, osl, oc,
     a_s, ph_s, sat_s, pig_s, cin, oc_in, dep, sol, cs, hs, hn, zup_s, zdn_s, zup_r, zdn_r, xe_s, xw_s, xe_r, xw_r,
     ps, pf, fs, fr, vsh, vsr, dpx, ops, mix, cw, ce, cu, cd,
-    uv, dls, dlr, pcs, pcr, scs, scr, wcs, wcr, pws, pwr, psr, fs2, fr2, fqs, fqr, ep, ews, ewr, ewx, n2s, n2r, solx, wst,
+    pst, psn, grown, kept, uv, dls, dlr, pcs, pcr, scs, scr, wcs, wcr, pws, pwr, psr, fs2, fr2, fqs, fqr, ep, ews, ewr, ewx, n2s, n2r, solx, wst,
     loc, ssems, rsems,
 ):
     b = lax.axis_index("grp")
@@ -37,7 +37,11 @@
     sides = ((has_w, west), (has_e, east), (has_s, south), (has_n, north))
     peers = [lax.rem(b + k, NG) for k in (2, 3, 1)]
 
-    loads = [pltpu.make_async_copy(c_hbm, cin, loc.at[0])]
+    cuts = (0, 6, 13, NT)
+    loads = []
+    for n in range(3):
+        part = pl.ds(32 * cuts[n], 32 * (cuts[n + 1] - cuts[n]))
+        loads.append(pltpu.make_async_copy(c_hbm.at[part], cin.at[part], loc.at[(0, 8, 9)[n]]))
     for n, (ref, dst) in enumerate(((pig_hbm, pig_s), (dep_hbm, dep), (sol_hbm, sol), (a_hbm, a_s), (ph_hbm, ph_s), (sat_hbm, sat_s))):
         loads.append(pltpu.make_async_copy(ref, dst, loc.at[1 + n]))
     for n, ref in enumerate((u_hbm, v_hbm, t_hbm, s_hbm, q_hbm)):
@@ -103,12 +107,7 @@
         def _():
             dpx[k] = jnp.zeros((4, 128), jnp.int32)
 
-    def publish(t):
-        pig = jnp.zeros((32, 128), F32)
-        for i in range(NT):
-            pig = pig + pig_s[i] * cs[t, i]
-        for r in range(NG):
-            ps[t, r] = pig[8 * r : 8 * r + 8]
+    def publish_light(t):
         pf[t, pl.ds(pl.multiple_of(b * 8, 8), 8), :] = ps[t, b]
         mine = pf.at[t, pl.ds(pl.multiple_of(b * 8, 8), 8), :]
         if t == 0:
@@ -153,7 +152,11 @@
                 send(dep_hbm, dpx.at[k ^ 1], f"dep{k ^ 1}", dev, there)
             send(sol_hbm, solx.at[0], "solw", east, has_e)
             send(sol_hbm, solx.at[1], "sols", north, has_n)
+    def publish_halos(t):
+        mine = pf.at[t, pl.ds(pl.multiple_of(b * 8, 8), 8), :]
         if t == 1:
+            for k, g in enumerate(peers):
+                send(ps.at[t, g], mine, "cols", {"grp": g}, whole=first(k, ps.at[t, 0:3]))
             sent([f"h{n}0" for n in range(6)])
         send(cs.at[t, :, pl.ds(24, 8), :], hs.at[t], f"h0{t}", north, has_n)
         send(cs.at[t, :, pl.ds(0, 8), :], hn.at[t], f"h1{t}", south, has_s)
@@ -173,9 +176,6 @@
 
         send(zup_s.at[t], zup_r.at[t], f"h4{t}", {"grp": b + 1}, b < NG - 1)
         send(zdn_s.at[t], zdn_r.at[t], f"h5{t}", {"grp": b - 1}, b > 0)
-        if t == 1:
-            for k, g in enumerate(peers):
-                send(ps.at[t, g], mine, "cols", {"grp": g}, whole=first(k, ps.at[t, 0:3]))
 
     def local_terms(t):
         def mixing(i, _):
@@ -306,9 +306,10 @@
 
     def await_light():
         arrived(pcr.at[0:3], "sums")
+
+    def await_sides():
         arrived(scr.at[0:3], "ssum", has_s)
         arrived(wcr.at[0:3], "wsum", has_w)
-        arrived(pf.at[1, 0:24], "cols")
         arrived(psr, "span", has_s)
         arrived(pwr, "wpan", has_w)
 
@@ -372,6 +373,9 @@
                 sal = window(fr2[r, 0], fr2[r, 1], 3)
                 quiet = window(fqr[r, 2], fqr[r, 3], 2)
                 got.append(band_ocean(ps[1, r], lambda g: pcr[g, r : r + 1], lambda g: pcr[g, NG + r : NG + r + 1], wide(sol[r : r + 1, :]), wide(dep[r : r + 1, :]), temp, sal, quiet, (u, v)))
+            arrived(pf.at[1, 0:24], "cols")
+            columns(1)
+            await_sides()
             edge = n2r[3]
             v = window(vsr[...], edge, 0)
             temp, sal, quiet = (window(n2r[n], edge, n + 1) for n in range(3))
@@ -426,6 +430,18 @@
             arrived(zdn_r.at[t], f"h5{t}")
             for i in range(NT):
                 cd[i, pl.ds(7, NG, stride=8), :] = zdn_r[t, i]
+
+    def pigment_terms():
+        sums = [jnp.zeros((32, 128), F32)] * 5
+        rows = [jnp.zeros((8, 128), F32)] * 2
+        for i in range(NT):
+            p = pig_s[i]
+            sums = [x + p * ref[i] for x, ref in zip(sums, (ce, cw, cd, cu, mix))]
+            rows = [x + p * ref[0, i] for x, ref in zip(rows, (hn, hs))]
+        for n, x in enumerate(sums):
+            pst[n] = x
+        for n, x in enumerate(rows):
+            psn[n] = x
 
     def update(t):
         got, west, south = forcing(t)
@@ -447,34 +463,61 @@
             warm = half * warm
             parw = half * par
             rows = pl.ds(8 * r, 8)
-
-            def one(i, _):
-                x = cs[t, i, rows, :]
-                up = cs[t, i, pl.ds(8 * r + 8, 8), :] if r < NG - 1 else hn[t, i]
-                dn = cs[t, i, pl.ds(8 * r - 8, 8), :] if r > 0 else hs[t, i]
-                grow = k0 + ph_s[i] * parw / (par + sat_s[i])
-                new = (
-                    grow * x
-                    + (b_e * ce[i, rows, :] + a_w * cw[i, rows, :])
-                    + (b_n * up + a_s_ * dn)
-                    + (d * cd[i, rows, :] + dm * cu[i, rows, :])
-                    + warm * mix[i, rows, :]
-                )
-                if t == STEPS - 1:
-                    oc[pl.ds(i * 32 + r, 8, stride=4), :] = new
-                else:
-                    cs[t + 1, i, rows, :] = new
-                return 0
-
-            lax.fori_loop(0, NT, one, 0, unroll=True)
-
-    loads[0].wait()
-    for i in range(NT):
-        for r in range(NG):
-            cs[0, i, pl.ds(8 * r, 8), :] = cin[pl.ds(i * 32 + r, 8, stride=4), :]
-    loads[1].wait()
-    publish(0)
-    for copy in loads[2:7] + [pltpu.make_async_copy(oc_in, oc_in, loc.at[7])]:
+            if t == 0:
+                new = k0 * ps[0, r] + (b_e * pst[0, rows, :] + a_w * pst[1, rows, :])
+                new = new + (b_n * (ps[0, r + 1] if r < NG - 1 else psn[0]) + a_s_ * (ps[0, r - 1] if r > 0 else psn[1]))
+                new = new + (d * pst[2, rows, :] + dm * pst[3, rows, :]) + warm * pst[4, rows, :]
+                for i in range(NT):
+                    photo = ph_s[i] * parw / (par + sat_s[i])
+                    grown[i, rows, :] = photo
+                    new = new + photo * (pig_s[i] * cs[t, i, rows, :])
+                ps[1, r] = new
+                for n, x in enumerate((k0, b_e, a_w, b_n, a_s_, d, dm, warm)):
+                    kept[r, n] = x
+            else:
+                stencil(t, r, (k0, b_e, a_w, b_n, a_s_, d, dm, warm), lambda i: ph_s[i] * parw / (par + sat_s[i]))
+        if t == 0:
+            publish_light(1)
+            for r in range(NG):
+                stencil(t, r, [kept[r, n] for n in range(8)], lambda i: grown[i, pl.ds(8 * r, 8), :])
+
+    def stencil(t, r, coefs, photo):
+        k0, b_e, a_w, b_n, a_s_, d, dm, warm = coefs
+        rows = pl.ds(8 * r, 8)
+
+        def one(i, _):
+            x = cs[t, i, rows, :]
+            up = cs[t, i, pl.ds(8 * r + 8, 8), :] if r < NG - 1 else hn[t, i]
+            dn = cs[t, i, pl.ds(8 * r - 8, 8), :] if r > 0 else hs[t, i]
+            new = (
+                (k0 + photo(i)) * x
+                + (b_e * ce[i, rows, :] + a_w * cw[i, rows, :])
+                + (b_n * up + a_s_ * dn)
+                + (d * cd[i, rows, :] + dm * cu[i, rows, :])
+                + warm * mix[i, rows, :]
+            )
+            if t == STEPS - 1:
+                oc[pl.ds(i * 32 + r, 8, stride=4), :] = new
+            else:
+                cs[t + 1, i, rows, :] = new
+            return 0
+
+        lax.fori_loop(0, NT, one, 0, unroll=True)
+
+    loads[3].wait()
+    pig = [jnp.zeros((8, 128), F32)] * NG
+    for n in range(3):
+        loads[n].wait()
+        for i in range(cuts[n], cuts[n + 1]):
+            for r in range(NG):
+                x = cin[pl.ds(i * 32 + r, 8, stride=4), :]
+                cs[0, i, pl.ds(8 * r, 8), :] = x
+                pig[r] = pig[r] + pig_s[i] * x
+    for r in range(NG):
+        ps[0, r] = pig[r]
+    publish_light(0)
+    publish_halos(0)
+    for copy in loads[4:9] + [pltpu.make_async_copy(oc_in, oc_in, loc.at[7])]:
         copy.wait()
     share_fixed()
     local_terms(0)
@@ -482,19 +525,19 @@
     share_state()
     openings()
     halos(0)
+    pigment_terms()
     arrived(fqr.at[0:3], "fixed")
     arrived(fr.at[0:3], "force")
     arrived(dlr.at[0:3], "edge")
     arrived(ewr, "u", has_w)
     arrived(vsr, "v", has_s)
     update(0)
-    publish(1)
+    publish_halos(1)
     local_terms(1)
     await_state()
     halos(1)
     await_light()
     update(1)
-    columns(1)
 
     sent()
 
@@ -534,13 +577,14 @@
             V((32, 128), F32), V((8, 128), F32),
             V((4, 4, 128), jnp.int32), V((5, NG, 8, 128), F32),
             V((NT, 32, 128), F32), V((NT, 32, 128), F32), V((NT, 32, 128), F32), V((NT, 32, 128), F32), V((NT, 32, 128), F32),
+            V((5, 32, 128), F32), V((2, 8, 128), F32), V((NT, 32, 128), F32), V((NG, 8, 8, 128), F32),
             V((NG, 2, 8, 128), F32), V((NG, 1, 128), F32), V((NG, 1, 128), F32), V((2, 8, 128), F32), V((NG, 8, 128), F32),
             V((2, 2, 128), F32), V((NG, 2, 128), F32), V((2, 2, 128), F32), V((NG, 2, 128), F32),
             V((8, 128), F32), V((8, 128), F32), V((8, 128), F32),
             V((NG, 2, 8, 128), F32), V((NG, 2, 8, 128), F32), V((NG, 4, 8, 128), F32), V((NG, 4, 8, 128), F32),
             V((32, 128), F32), V((NG, 8, 128), F32), V((NG, 8, 128), F32), V((NG, 8, 128), F32),
             V((NG, 4, 8, 128), F32), V((4, 8, 128), F32), V((2, 4, 128), F32), V((6, 16, 128), F32),
-            D((8,)), D((len(SEND),)), D((len(RECV),)),
+            D((10,)), D((len(SEND),)), D((len(RECV),)),
         ],
         compiler_params=pltpu.CompilerParams(collective_id=0, has_side_effects=True, vmem_limit_bytes=16 << 20),
     )(*[pltpu.with_memory_space_constraint(x, pltpu.HBM) for x in (*fields, c.reshape(NT * 32, 128), dep, sol, rates, photo, satur, pig)])

time: 30.9 us -> 30.7 us (level)
  no operation moved by 1% of the time
where the time goes in v6:
time: 30.7 us; the launch traced here: 30.5 us
  Pallas kernels  29.9 us (97%)
  between operations  0.64 us (2%)
    pallas_call x1, Pallas kernels, per_device(): pl.pallas_call(functools.partial(kernel, nx, ny), out_shape=(col, col, co...  29.1 us
    pallas_call x1, Pallas kernels, per_device(): pl.pallas_call(write_out, out_shape=(col, col, col, col, jax.ShapeDtypeSt...  0.79 us

profile of v6, /device:TPU:1, one launch (start us, length us, event | category | flops | bytes accessed | tf_op | source)
XLA Modules:
  0.0 30.5 jit_solution(6596597525815455859)
XLA Ops:
  0.6 29.1 %shard_map.155 = (f32[32,128]{1,0:T(8,128)S(1)}, f32[32,128]{1,0:T(8,128)S(1)}, f32[32,128]{1,0:T(8,128)S(1)}, f32[32,128]{1,0:T(8,128)S(1)}, f32[608,128]{1,0:T(8,128)S(1)}) custom-call(f32[32,128]{1,0:T(8,128)} %bitcast.20, f32[32,128]{1,0:T(8,128)} %bitcast.21, f32[32,128]{1,0:T(8,128)} %bitcast.22, f32[32,128]{1,0:T(8,128)} %bitcast.23, ...), custom_call_target="tpu_custom_call" | custom-call | tf_op jit(solution)/shard_map/pallas_call | solution.py:564
  29.7 0.8 %shard_map.156 = (f32[32,128]{1,0:T(8,128)}, f32[32,128]{1,0:T(8,128)}, f32[32,128]{1,0:T(8,128)}, f32[32,128]{1,0:T(8,128)}, f32[608,128]{1,0:T(8,128)}) custom-call(f32[32,128]{1,0:T(8,128)S(1)} %get-tuple-element.15.refs_0_, f32[32,128]{1,0:T(8,128)S(1)} %get-tuple-element.16.refs_1_, f32[32,128]{1,0:T(8,128)S(1)} %get-tuple-element.17.refs_2_, ...), custom_call_target="tpu_custom_call" | custom-call | tf_op jit(solution)/shard_map/pallas_call | solution.py:591

commit v7 on v6

--- a/solution.py
+++ b/solution.py
@@ -243,9 +243,6 @@
             dls[0] = jnp.zeros((1, 128), F32)
             for g in range(1, NG):
                 dls[g] = face[8 * g - 1 : 8 * g]
-            for k, g in enumerate(peers):
-                send(fs.at[g], fr.at[b], "force", {"grp": g}, whole=first(k, fs.at[0:3]))
-                send(dls.at[g], dlr.at[b], "edge", {"grp": g}, whole=first(k, dls.at[0:3]))
             vsh[...] = v
             for g in range(NG):
                 send(vsh.at[pl.ds(8 * g, 8), :], vsr, "v", {"grp": g, **north}, jnp.logical_and(b == NG - 1, has_n), first(g, vsh))
@@ -255,6 +252,9 @@
             ep[...] = pack
             for g in range(NG):
                 send(ep.at[8 * g : 8 * g + 8], ewr.at[b], "u", {"grp": g, **east}, has_e, first(g, ep))
+            for k, g in enumerate(peers):
+                send(fs.at[g], fr.at[b], "force", {"grp": g}, whole=first(k, fs.at[0:3]))
+                send(dls.at[g], dlr.at[b], "edge", {"grp": g}, whole=first(k, dls.at[0:3]))
             fr[b] = fs[b]
             dlr[b] = dls[b]
         ou[...] = u

time: 30.7 us -> 30.9 us (level)
  no operation moved by 1% of the time
where the time goes in v7:
time: 30.9 us; the launch traced here: 30.7 us
  Pallas kernels  30 us (97%)
  between operations  0.64 us (2%)
    pallas_call x1, Pallas kernels, per_device(): pl.pallas_call(functools.partial(kernel, nx, ny), out_shape=(col, col, co...  29.2 us
    pallas_call x1, Pallas kernels, per_device(): pl.pallas_call(write_out, out_shape=(col, col, col, col, jax.ShapeDtypeSt...  0.79 us

profile of v7, /device:TPU:1, one launch (start us, length us, event | category | flops | bytes accessed | tf_op | source)
XLA Modules:
  0.0 30.7 jit_solution(3581520416618385760)
XLA Ops:
  0.6 29.2 %shard_map.155 = (f32[32,128]{1,0:T(8,128)S(1)}, f32[32,128]{1,0:T(8,128)S(1)}, f32[32,128]{1,0:T(8,128)S(1)}, f32[32,128]{1,0:T(8,128)S(1)}, f32[608,128]{1,0:T(8,128)S(1)}) custom-call(f32[32,128]{1,0:T(8,128)} %bitcast.20, f32[32,128]{1,0:T(8,128)} %bitcast.21, f32[32,128]{1,0:T(8,128)} %bitcast.22, f32[32,128]{1,0:T(8,128)} %bitcast.23, ...), custom_call_target="tpu_custom_call" | custom-call | tf_op jit(solution)/shard_map/pallas_call | solution.py:564
  29.9 0.8 %shard_map.156 = (f32[32,128]{1,0:T(8,128)}, f32[32,128]{1,0:T(8,128)}, f32[32,128]{1,0:T(8,128)}, f32[32,128]{1,0:T(8,128)}, f32[608,128]{1,0:T(8,128)}) custom-call(f32[32,128]{1,0:T(8,128)S(1)} %get-tuple-element.15.refs_0_, f32[32,128]{1,0:T(8,128)S(1)} %get-tuple-element.16.refs_1_, f32[32,128]{1,0:T(8,128)S(1)} %get-tuple-element.17.refs_2_, ...), custom_call_target="tpu_custom_call" | custom-call | tf_op jit(solution)/shard_map/pallas_call | solution.py:591
